TPU v7x, 32 devices: a whole 2x2x4 slice. The times are simulated.
32 devices in a mesh: rev: 8 (over y, x, core), row: 4 (over z).
Axes of the slice: x: 2, y: 2, z: 4, core: 2. Of those that a mesh axis runs over, the one named last changes fastest.
Arguments:
- fields: bfloat16 [8, 16, 1024, 1024], P('rev', None, 'row'), may hold values from -6 to 6
- out_grads: bfloat16 [8, 16, 1024, 1024], P('rev', None, 'row'), may hold values from -6 to 6
- partner: int32 [8], replicated, may hold values from 0 to 7, as said below
- kept_blocks: int32 [8], replicated, may hold values from 1 to 8
- weight_in: float32 [1, 2, 32, 16], replicated, may hold values from -0.75 to 0.75
- bias_in: float32 [1, 2, 16], replicated, may hold values from -3 to 3
- weight_out: float32 [1, 2, 16, 16], replicated, may hold values from -1 to 1
Outputs:
- field_grads: bfloat16 [8, 16, 1024, 1024], P('rev', None, 'row')
- grad_weight_in: float32 [1, 2, 32, 16], replicated
- grad_bias_in: float32 [1, 2, 16], replicated
- grad_weight_out: float32 [1, 2, 16, 16], replicated
- grad_bias_out: float32 [1, 2, 16], replicated
Inputs may be any that keep to these rules, and one draw needn't show every extreme that they name: partner[partner[r]] = r and partner[r] != r for every revision r; some revision r has partner[r] = (r + 4) mod 8.
All inputs are finite; a program needn't handle non-finite values.
Results may differ from a plain program's by a relative error of at most 0.01.
Values may be sent and summed in bfloat16 or wider, within the bound.
A program may use at most 128 MiB of HBM per device.

v0:
```python
import math

import jax
import jax.numpy as jnp
from jax import lax
from jax.sharding import PartitionSpec as P

NH = 1024
NW = 1024
KX = 128
MB = 16
KY = 256


HIGHEST = lax.Precision.HIGHEST


def column_tables(n_cols, n_keep):
    col_index = jnp.arange(n_cols, dtype=jnp.int32)[:, None]
    freq_index = jnp.arange(n_keep, dtype=jnp.int32)[None, :]
    phases = col_index * freq_index % n_cols
    angles = phases.astype(jnp.float32) * (2.0 * math.pi / n_cols)
    return (jnp.cos(angles).astype(jnp.bfloat16), jnp.sin(angles).astype(jnp.bfloat16))


def row_tables(n_rows, n_keep):
    row_index = jnp.arange(n_rows, dtype=jnp.int32)[None, :]
    slot_index = jnp.arange(n_keep, dtype=jnp.int32)
    signed = jnp.where(slot_index < n_keep // 2, slot_index, slot_index - n_keep + n_rows)
    phases = signed[:, None] * row_index % n_rows
    angles = phases.astype(jnp.float32) * (2.0 * math.pi / n_rows)
    return (jnp.cos(angles).astype(jnp.bfloat16), jnp.sin(angles).astype(jnp.bfloat16))


def keep_mask(kept_count, col_index, n_keep):
    slot_index = jnp.arange(n_keep, dtype=jnp.int32)
    row_extent = jnp.where(slot_index < n_keep // 2, slot_index, n_keep - slot_index)
    extent = jnp.maximum(col_index[:, None], row_extent[None, :])
    return (extent < kept_count * MB).astype(jnp.float32)


def complex_layer(weights, biases, real_part, imag_part):

    def mixing(matrix, values):
        return jnp.einsum("bio,bipq->bopq", matrix, values, precision=HIGHEST)

    weight_real = weights[:, 0]
    weight_imag = weights[:, 1]
    out_real = (
        mixing(weight_real, real_part)
        - mixing(weight_imag, imag_part)
        + biases[:, 0, :, None, None]
    )
    out_imag = (
        mixing(weight_imag, real_part)
        + mixing(weight_real, imag_part)
        + biases[:, 1, :, None, None]
    )
    return (out_real, out_imag)


def spectral_mlp(params, own_spec, other_spec):
    weight_in, bias_in, weight_out, bias_out = params
    blocks = weight_in.shape[0]
    block_width = own_spec.shape[1] // blocks
    trailing = own_spec.shape[2:]

    def split_blocks(spectrum):
        return spectrum.reshape((2, blocks, block_width) + trailing)

    joined = jnp.concatenate([split_blocks(own_spec), split_blocks(other_spec)], axis=2)
    hidden_real, hidden_imag = complex_layer(weight_in, bias_in, joined[0], joined[1])
    hidden_real = jax.nn.gelu(hidden_real, approximate=True)
    hidden_imag = jax.nn.gelu(hidden_imag, approximate=True)
    out_real, out_imag = complex_layer(weight_out, bias_out, hidden_real, hidden_imag)
    return jnp.stack([out_real, out_imag]).reshape((2, blocks * block_width) + trailing)


def mlp_backward(params, own_spec, other_spec, cotangent):
    unused, pullback = jax.vjp(spectral_mlp, params, own_spec, other_spec)
    return pullback(cotangent)


def column_pass(field, col_cos, col_sin):
    channels, n_rows, n_cols = field.shape
    flattened = field.reshape(channels * n_rows, n_cols)
    real_cols = jnp.dot(flattened, col_cos, preferred_element_type=jnp.float32)
    imag_cols = -jnp.dot(flattened, col_sin, preferred_element_type=jnp.float32)
    return jnp.stack([real_cols, imag_cols]).astype(jnp.bfloat16).reshape(2, channels, n_rows, -1)


def row_spectrum(column_spec, row_cos, row_sin):
    with_cos = jnp.einsum("schk,jh->sckj", column_spec, row_cos, preferred_element_type=jnp.float32)
    with_sin = jnp.einsum("schk,jh->sckj", column_spec, row_sin, preferred_element_type=jnp.float32)
    real_part = with_cos[0] + with_sin[1]
    imag_part = with_cos[1] - with_sin[0]
    return jnp.stack([real_part, imag_part]) * (1.0 / math.sqrt(NH * NW))


def inverse_rows(total, row_cos, row_sin):
    with_cos = jnp.einsum("sckj,jh->schk", total, row_cos, preferred_element_type=jnp.float32)
    with_sin = jnp.einsum("sckj,jh->schk", total, row_sin, preferred_element_type=jnp.float32)
    real_part = with_cos[0] - with_sin[1]
    imag_part = with_sin[0] + with_cos[1]
    return jnp.stack([real_part, imag_part]).astype(jnp.bfloat16)


def inverse_cols(rows_spec, col_cos, col_sin):
    channels, n_rows, n_keep = rows_spec.shape[1:]
    real_rows = rows_spec[0].reshape(channels * n_rows, n_keep)
    imag_rows = rows_spec[1].reshape(channels * n_rows, n_keep)
    result_real = jnp.einsum("hk,wk->hw", real_rows, col_cos, preferred_element_type=jnp.float32)
    result_imag = jnp.einsum("hk,wk->hw", imag_rows, col_sin, preferred_element_type=jnp.float32)
    field = (result_real - result_imag) * (1.0 / math.sqrt(NH * NW))
    return field.astype(jnp.bfloat16).reshape(channels, n_rows, -1)


def local(fields, out_grads, partner, kept_blocks, weight_in, bias_in, weight_out):
    col_cos, col_sin = column_tables(NW, KX)
    row_cos, row_sin = row_tables(NH, KY)
    own_rev = lax.axis_index("rev")
    row_rank = lax.axis_index("row")
    local_cols = KX // lax.axis_size("row")
    field_cols = column_pass(fields[0], col_cos, col_sin)
    grad_cols = column_pass(out_grads[0], col_cos, col_sin)
    spectra = row_spectrum(
        lax.all_to_all(field_cols, "row", split_axis=3, concat_axis=2, tiled=True), row_cos, row_sin
    )
    grad_spec = row_spectrum(
        lax.all_to_all(grad_cols, "row", split_axis=3, concat_axis=2, tiled=True), row_cos, row_sin
    )

    def route(spectrum):
        target = partner[own_rev]
        slot_array = jnp.zeros((lax.axis_size("rev"),) + spectrum.shape, spectrum.dtype)
        slot_array = lax.dynamic_update_index_in_dim(slot_array, spectrum, target, 0)
        received = lax.all_to_all(slot_array, "rev", split_axis=0, concat_axis=0, tiled=True)
        return lax.dynamic_index_in_dim(received, target, 0, keepdims=False)

    partner_spec = route(spectra.astype(jnp.bfloat16)).astype(jnp.float32)
    col_index = row_rank * local_cols + jnp.arange(local_cols, dtype=jnp.int32)
    keep_local = keep_mask(kept_blocks[own_rev], col_index, KY)
    params = (weight_in, bias_in, weight_out, jnp.zeros_like(bias_in))
    param_grads, own_grads, other_grads = mlp_backward(
        params, spectra, partner_spec, grad_spec * keep_local[None, None]
    )
    returned = route(other_grads.astype(jnp.bfloat16)).astype(jnp.float32)
    total = (own_grads + returned).astype(jnp.bfloat16)
    rows_spec = inverse_rows(total, row_cos, row_sin)
    field_grads = inverse_cols(
        lax.all_to_all(rows_spec, "row", split_axis=2, concat_axis=3, tiled=True), col_cos, col_sin
    )
    summed = lax.psum(
        (param_grads[0], param_grads[1], param_grads[2], param_grads[3]), ("rev", "row")
    )
    grad_scale = 1.0 / math.sqrt(lax.axis_size("rev") * KX * KY)
    return (
        field_grads[None],
        summed[0] * grad_scale,
        summed[1] * grad_scale,
        summed[2] * grad_scale,
        summed[3] * grad_scale,
    )


def solution(mesh):
    placed = (P("rev", None, "row", None), P("rev", None, "row", None), P(), P(), P(), P(), P())
    return jax.shard_map(
        local,
        mesh=mesh,
        in_specs=placed,
        out_specs=(P("rev", None, "row", None), P(), P(), P(), P()),
        check_vma=False,
    )
```

profile of v0, /device:TPU:0, one launch (start us, length us, event | category | flops | bytes accessed | tf_op | source)
XLA Modules:
  0.0 385.1 jit_solution(9175087213200670544)
XLA Ops:
  0.6 8.1 %fusion.1 = bf16[128,4096]{1,0:T(8,128)(2,1)S(1)} fusion(bf16[4096,1024]{1,0:T(8,128)(2,1)} %bitcast.364), kind=kOutput, calls=%fused_computation.4 | convolution fusion | flops 1076756480 | bytes 9437184 | tf_op jit(solution)/shard_map/dot_general | solution.py:88
  8.8 4.6 %convolution_convert_fusion = bf16[128,4096]{1,0:T(8,128)(2,1)S(1)} fusion(bf16[4096,1024]{1,0:T(8,128)(2,1)S(1)} %bitcast.365), kind=kOutput, calls=%fused_computation.5 | convolution fusion | flops 1076232192 | bytes 9437184 | tf_op jit(solution)/shard_map/dot_general | solution.py:87
  13.9 1.5 pad_maximum_fusion.1
  15.4 6.5 %all-to-all-start.1 = ((bf16[2,16,256,128]{2,1,0,3:T(8,128)(2,1)}), bf16[2,16,256,128]{2,1,0,3:T(8,128)(2,1)S(1)}, u32[]{:S(2)}, u32[]{:S(2)}) async-start(bf16[2,16,256,128]{2,1,0,3:T(8,128)(2,1)} %pad_maximum_fusion.1), calls=%async_computation.1 | async-start | bytes 4194304 | tf_op jit(solution)/shard_map/all_to_all | solution.py:127
  21.9 8.0 %fusion = bf16[128,4096]{1,0:T(8,128)(2,1)S(1)} fusion(bf16[4096,1024]{1,0:T(8,128)(2,1)} %bitcast.366), kind=kOutput, calls=%fused_computation.3 | convolution fusion | flops 1076756480 | bytes 9437184 | tf_op jit(solution)/shard_map/dot_general | solution.py:88
  30.2 8.0 %convolution_convert_fusion.1 = bf16[128,4096]{1,0:T(8,128)(2,1)S(1)} fusion(bf16[4096,1024]{1,0:T(8,128)(2,1)} %bitcast.367), kind=kOutput, calls=%fused_computation.6 | convolution fusion | flops 1076232192 | bytes 9437184 | tf_op jit(solution)/shard_map/dot_general | solution.py:87
  38.4 1.6 pad_maximum_fusion
  40.0 30.2 %all-to-all-done.1 = bf16[2,16,256,128]{2,1,0,3:T(8,128)(2,1)S(1)} async-done(((bf16[2,16,256,128]{2,1,0,3:T(8,128)(2,1)}), bf16[2,16,256,128]{2,1,0,3:T(8,128)(2,1)S(1)}, u32[]{:S(2)}, u32[]{:S(2)}) %all-to-all-start.1) | async-done | bytes 2097184 | tf_op jit(solution)/shard_map/all_to_all | solution.py:127
  70.1 1.3 copy-done
  71.4 4.0 %all-to-all-start = ((bf16[2,16,256,128]{2,1,0,3:T(8,128)(2,1)}), bf16[2,16,256,128]{2,1,0,3:T(8,128)(2,1)S(1)}, u32[]{:S(2)}, u32[]{:S(2)}) async-start(bf16[2,16,256,128]{2,1,0,3:T(8,128)(2,1)} %pad_maximum_fusion), calls=%async_computation | async-start | bytes 4194304 | tf_op jit(solution)/shard_map/all_to_all | solution.py:130
  78.0 4.5 %copy.142 = bf16[2,16,256,4,32]{2,3,4,1,0:T(4,128)(2,1)} copy(bf16[2,16,256,4,32]{2,1,0,4,3:T(8,128)(2,1)} %bitcast.346) | data formatting | bytes 4194304 | tf_op jit(solution)/shard_map/all_to_all | solution.py:127
  82.5 4.4 %all_to_all.50 = bf16[2,16,1024,32]{2,3,1,0:T(8,128)(2,1)} reshape(bf16[2,16,4,256,32]{3,2,4,1,0:T(4,128)(2,1)} %bitcast.347) | data formatting | bytes 4194304 | tf_op jit(solution)/shard_map/all_to_all | solution.py:127
  87.0 6.3 %fusion.88 = f32[2,16,32,256]{3,2,1,0:T(8,128)S(1)} fusion(bf16[2,16,1024,32]{2,3,1,0:T(8,128)(2,1)} %all_to_all.50, s32[256]{0:T(256)S(1)} %compare_select_fusion.1), kind=kOutput, calls=%fused_computation.150 | convolution fusion | flops 540803072 | bytes 3146752 | tf_op jit(solution)/shard_map/schk,jh->sckj/dot_general | solution.py:94
  93.2 4.5 %fusion.93 = f32[2,16,32,256]{3,2,1,0:T(8,128)S(1)} fusion(bf16[2,16,1024,32]{2,3,1,0:T(8,128)(2,1)S(1)} %copy-done.4, s32[256]{0:T(256)S(1)} %compare_select_fusion.1), kind=kOutput, calls=%fused_computation.152 | convolution fusion | flops 540803072 | bytes 3146752 | tf_op jit(solution)/shard_map/schk,jh->sckj/dot_general | solution.py:93
  97.9 2.5 broadcast.158.clone
  101.4 21.7 %all-to-all-done = bf16[2,16,256,128]{2,1,0,3:T(8,128)(2,1)S(1)} async-done(((bf16[2,16,256,128]{2,1,0,3:T(8,128)(2,1)}), bf16[2,16,256,128]{2,1,0,3:T(8,128)(2,1)S(1)}, u32[]{:S(2)}, u32[]{:S(2)}) %all-to-all-start) | async-done | bytes 2097184 | tf_op jit(solution)/shard_map/all_to_all | solution.py:130
  123.1 4.6 %all-to-all-start.2 = ((bf16[8,2,16,32,256]{4,3,2,1,0:T(8,128)(2,1)}), bf16[8,2,16,32,256]{4,3,2,1,0:T(8,128)(2,1)}, u32[]{:S(2)}, u32[]{:S(2)}) async-start(bf16[8,2,16,32,256]{4,3,2,1,0:T(8,128)(2,1)} %fusion.62), calls=%async_computation.2 | async-start | bytes 8388608 | tf_op jit(solution)/shard_map/all_to_all | solution.py:137
  129.1 3.0 copy.143
  132.0 3.4 all_to_all.46
  136.5 4.5 %fusion.90 = f32[2,16,32,256]{3,2,1,0:T(8,128)S(1)} fusion(bf16[2,16,1024,32]{2,3,1,0:T(8,128)(2,1)S(1)} %all_to_all.46, s32[256]{0:T(256)S(1)} %compare_select_fusion.1), kind=kOutput, calls=%fused_computation.151 | convolution fusion | flops 540803072 | bytes 3146752 | tf_op jit(solution)/shard_map/schk,jh->sckj/dot_general | solution.py:94
  141.1 4.5 %fusion.95 = f32[2,16,32,256]{3,2,1,0:T(8,128)S(1)} fusion(bf16[2,16,1024,32]{2,3,1,0:T(8,128)(2,1)S(1)} %all_to_all.46, s32[256]{0:T(256)S(1)} %compare_select_fusion.1), kind=kOutput, calls=%fused_computation.153 | convolution fusion | flops 540803072 | bytes 3146752 | tf_op jit(solution)/shard_map/schk,jh->sckj/dot_general | solution.py:93
  147.0 1.7 fusion.106
  148.7 1.7 fusion.108
  150.4 26.4 %all-to-all-done.2 = bf16[8,2,16,32,256]{4,3,2,1,0:T(8,128)(2,1)} async-done(((bf16[8,2,16,32,256]{4,3,2,1,0:T(8,128)(2,1)}), bf16[8,2,16,32,256]{4,3,2,1,0:T(8,128)(2,1)}, u32[]{:S(2)}, u32[]{:S(2)}) %all-to-all-start.2) | async-done | bytes 4194336 | tf_op jit(solution)/shard_map/all_to_all | solution.py:137
  178.7 1.7 fusion.39
  180.4 1.3 fusion.41
  181.7 1.3 fusion.5
  183.0 1.3 fusion.202
  186.4 1.3 fusion.4
  187.7 1.3 fusion.201
  191.0 2.5 fusion.28
  194.1 51.6 %all_to_all.61 = bf16[8,2,16,32,256]{4,3,2,1,0:T(8,128)(2,1)S(1)} all-to-all(bf16[8,2,16,32,256]{4,3,2,1,0:T(8,128)(2,1)S(1)} %fusion.64), channel_id=1, replica_groups=mesh['rev'=8,'row'=4] {'rev'}, dimensions={0} | all-to-all | bytes 8388608 | tf_op jit(solution)/shard_map/all_to_all | solution.py:137
  245.8 4.6 %convolution_bitcast_fusion = f32[2,16,1024,32]{2,3,1,0:T(8,128)S(1)} fusion(bf16[2,16,32,256]{3,2,1,0:T(8,128)(2,1)S(1)} %fusion.22, s32[256]{0:T(256)S(1)} %compare_select_fusion.1), kind=kOutput, calls=%fused_computation.7 | convolution fusion | flops 540803072 | bytes 4719616 | tf_op jit(solution)/shard_map/sckj,jh->schk/dot_general | solution.py:102
  250.4 4.5 %convolution_bitcast_fusion.1 = f32[2,16,1024,32]{2,3,1,0:T(8,128)S(1)} fusion(bf16[2,16,32,256]{3,2,1,0:T(8,128)(2,1)S(1)} %fusion.22, s32[256]{0:T(256)S(1)} %compare_select_fusion.1), kind=kOutput, calls=%fused_computation.8 | convolution fusion | flops 540803072 | bytes 4719616 | tf_op jit(solution)/shard_map/sckj,jh->schk/dot_general | solution.py:101
  254.9 1.2 fusion.3
  256.1 1.5 pad_maximum_fusion.2
  257.6 12.5 %copy.77 = bf16[2,16,1024,32]{3,1,0,2:T(8,128)(2,1)} copy(bf16[2,16,1024,32]{2,3,1,0:T(8,128)(2,1)} %pad_maximum_fusion.2) | data formatting | bytes 4194304 | tf_op jit(solution)/shard_map/stack | solution.py:105
  270.1 10.7 %reshape.381 = bf16[4,2,131072]{2,1,0:T(2,128)(2,1)} reshape(bf16[1024,2,16,32]{3,2,1,0:T(8,128)(2,1)} %bitcast.340) | data formatting | bytes 4194304
  280.8 4.4 %all-to-all-start.4 = ((bf16[4,2,131072]{2,1,0:T(2,128)(2,1)}), bf16[4,2,131072]{2,1,0:T(2,128)(2,1)}, u32[]{:S(2)}, u32[]{:S(2)}) async-start(bf16[4,2,131072]{2,1,0:T(2,128)(2,1)} %reshape.381), calls=%async_computation.4 | async-start | bytes 4194304 | tf_op jit(solution)/shard_map/all_to_all | solution.py:151
  285.3 1.4 convolution_bitcast_fusion.2
  286.7 1.4 convolution_bitcast_fusion.4
  288.1 1.4 fusion.9
  289.5 1.4 fusion.11
  295.2 57.3 %all-reduce.10 = (f32[1,2,32,16]{2,3,1,0:T(8,128)S(1)}, f32[1,2,16]{2,1,0:T(2,128)S(1)}, f32[1,2,16,16]{2,3,1,0:T(8,128)S(1)}, f32[1,2,16]{2,1,0:T(2,128)S(1)}) all-reduce(f32[1,2,32,16]{2,3,1,0:T(8,128)S(1)} %pad_add_fusion.2, f32[1,2,16]{2,1,0:T(2,128)S(1)} %pad_add_fusion.4, ...), channel_id=1, replica_groups=mesh['rev'=8,'row'=4] {'rev','row'}, use_global_device_ids=true, to_apply=%region_0.1 | all-reduce | flops 1600 | bytes 12800 | tf_op jit(solution)/shard_map/psum | solution.py:153
  354.4 7.3 %reshape.382 = bf16[1024,2,16,32]{3,2,1,0:T(8,128)(2,1)} reshape(bf16[4,2,131072]{2,1,0:T(2,128)(2,1)} %all-to-all-done.4) | data formatting | bytes 4194304
  361.8 10.9 %copy.78 = bf16[2,16,4,256,32]{3,1,4,2,0:T(8,128)(2,1)S(1)} copy(bf16[2,16,4,256,32]{4,1,0,3,2:T(8,128)(2,1)} %bitcast.341) | data formatting | bytes 4194304 | tf_op jit(solution)/shard_map/all_to_all | solution.py:151
  373.8 4.4 %fusion.110 = f32[4096,1024]{1,0:T(8,128)S(1)} fusion(bf16[4096,128]{0,1:T(8,128)(2,1)S(1)} %bitcast.349), kind=kOutput, calls=%fused_computation.171 | convolution fusion | flops 1075707904 | bytes 17825792 | tf_op jit(solution)/shard_map/hk,wk->hw/dot_general | solution.py:112
  378.2 6.5 %multiply_convert_fusion = bf16[4096,1024]{1,0:T(8,128)(2,1)} fusion(f32[4096,1024]{1,0:T(8,128)S(1)} %fusion.110, bf16[4096,128]{0,1:T(8,128)(2,1)S(1)} %bitcast.343), kind=kOutput, calls=%fused_computation | convolution fusion | flops 1088290816 | bytes 26214400 | tf_op jit(solution)/shard_map/hk,wk->hw/dot_general | solution.py:113
  (83 shorter events, 19.9 us)
Async XLA Ops:
  0.6 8.1 %copy-start.18 = (bf16[1,16,256,1024]{3,2,1,0:T(8,128)(2,1)S(1)}, bf16[1,16,256,1024]{3,2,1,0:T(8,128)(2,1)}, u32[]{:S(2)}) copy-start(bf16[1,16,256,1024]{3,2,1,0:T(8,128)(2,1)} %param.7) | copy-start | bytes 25165828
  15.4 54.7 %all-to-all-start.1 = ((bf16[2,16,256,128]{2,1,0,3:T(8,128)(2,1)}), bf16[2,16,256,128]{2,1,0,3:T(8,128)(2,1)S(1)}, u32[]{:S(2)}, u32[]{:S(2)}) async-start(bf16[2,16,256,128]{2,1,0,3:T(8,128)(2,1)} %pad_maximum_fusion.1), calls=%async_computation.1 | async-start | bytes 4194304 | tf_op jit(solution)/shard_map/all_to_all | solution.py:127
  40.0 35.5 %copy-start.19 = (s32[8]{0:T(128)S(1)}, s32[8]{0:T(128)}, u32[]{:S(2)}) copy-start(s32[8]{0:T(128)} %param.9) | copy-start | bytes 100
  70.1 1.3 copy-start
  71.4 51.7 %all-to-all-start = ((bf16[2,16,256,128]{2,1,0,3:T(8,128)(2,1)}), bf16[2,16,256,128]{2,1,0,3:T(8,128)(2,1)S(1)}, u32[]{:S(2)}, u32[]{:S(2)}) async-start(bf16[2,16,256,128]{2,1,0,3:T(8,128)(2,1)} %pad_maximum_fusion), calls=%async_computation | async-start | bytes 4194304 | tf_op jit(solution)/shard_map/all_to_all | solution.py:130
  87.0 6.3 %copy-start.4 = (bf16[2,16,1024,32]{2,3,1,0:T(8,128)(2,1)S(1)}, bf16[2,16,1024,32]{2,3,1,0:T(8,128)(2,1)}, u32[]{:S(2)}) copy-start(bf16[2,16,1024,32]{2,3,1,0:T(8,128)(2,1)} %all_to_all.50) | copy-start | bytes 6291460
  101.4 26.3 %copy-start.20 = (s32[8]{0:T(128)S(1)}, s32[8]{0:T(128)}, u32[]{:S(2)}) copy-start(s32[8]{0:T(128)} %param.10) | copy-start | bytes 100
  101.4 27.5 %copy-start.17 = (f32[1,2,16]{2,1,0:T(2,128)S(1)}, f32[1,2,16]{2,1,0:T(2,128)}, u32[]{:S(2)}) copy-start(f32[1,2,16]{2,1,0:T(2,128)} %param.12) | copy-start | bytes 388
  123.1 53.7 %all-to-all-start.2 = ((bf16[8,2,16,32,256]{4,3,2,1,0:T(8,128)(2,1)}), bf16[8,2,16,32,256]{4,3,2,1,0:T(8,128)(2,1)}, u32[]{:S(2)}, u32[]{:S(2)}) async-start(bf16[8,2,16,32,256]{4,3,2,1,0:T(8,128)(2,1)} %fusion.62), calls=%async_computation.2 | async-start | bytes 8388608 | tf_op jit(solution)/shard_map/all_to_all | solution.py:137
  145.8 1.2 copy-start.16
  147.0 1.7 copy-start.1
  147.0 30.9 %copy-start.3 = (f32[2,1,16,32,256]{4,3,2,1,0:T(8,128)S(1)}, f32[2,1,16,32,256]{4,3,2,1,0:T(8,128)}, u32[]{:S(2)}) copy-start(f32[2,1,16,32,256]{4,3,2,1,0:T(8,128)} %maximum_multiply_fusion.1) | copy-start | bytes 3145732
  178.0 0.7 copy-start.15
  180.4 2.6 copy-start.5
  180.4 2.6 copy-start.14
  183.0 2.3 copy-start.9
  185.3 2.3 copy-start.7
  185.3 2.3 copy-start.13
  187.6 2.3 copy-start.11
  280.8 73.6 %all-to-all-start.4 = ((bf16[4,2,131072]{2,1,0:T(2,128)(2,1)}), bf16[4,2,131072]{2,1,0:T(2,128)(2,1)}, u32[]{:S(2)}, u32[]{:S(2)}) async-start(bf16[4,2,131072]{2,1,0:T(2,128)(2,1)} %reshape.381), calls=%async_computation.4 | async-start | bytes 4194304 | tf_op jit(solution)/shard_map/all_to_all | solution.py:151
  286.7 4.3 %copy-start.8 = (f32[16,32,256]{2,1,0:T(8,128)S(1)}, f32[16,32,256]{2,1,0:T(8,128)}, u32[]{:S(2)}) copy-start(f32[16,32,256]{2,1,0:T(8,128)} %get-tuple-element.36) | copy-start | bytes 1572868
  286.7 4.3 %copy-start.12 = (f32[32,256,16]{1,2,0:T(8,128)S(1)}, f32[32,256,16]{1,2,0:T(8,128)}, u32[]{:S(2)}) copy-start(f32[32,256,16]{1,2,0:T(8,128)} %copy-done.11) | copy-start | bytes 1572868
  288.1 3.9 %copy-start.6 = (f32[16,32,256]{2,1,0:T(8,128)S(1)}, f32[16,32,256]{2,1,0:T(8,128)}, u32[]{:S(2)}) copy-start(f32[16,32,256]{2,1,0:T(8,128)} %get-tuple-element.37) | copy-start | bytes 1572868
  288.1 3.9 %copy-start.10 = (f32[32,256,16]{1,2,0:T(8,128)S(1)}, f32[32,256,16]{1,2,0:T(8,128)}, u32[]{:S(2)}) copy-start(f32[32,256,16]{1,2,0:T(8,128)} %copy-done.9) | copy-start | bytes 1572868
  289.5 3.5 copy-start.2
where the time goes:
time: 393 us; the launch traced here: 385 us
  blocking collectives  109 us (28%)
  matrix products  93.7 us (24%)
  waiting for transfers between devices  78.3 us (20%)
  local copies, waits for them, and re-layouts  65.6 us (17%)
  starting transfers between devices  19.5 us (5%)
  other arithmetic  14.8 us (4%)
  between operations  4.32 us (1%)
    psum x1, blocking collectives, local(): lax.psum((param_grads[0], param_grads[1], param_grads[2], param_grads[3])...  57.3 us
    all_to_all x1, blocking collectives, route(): lax.all_to_all(slot_array, 'rev', split_axis=0, concat_axis=0, tiled=True)  51.6 us
    all_to_all x1, waiting for transfers between devices, local(): lax.all_to_all(field_cols, 'row', split_axis=3, concat_axis=2, tiled=True)  30.2 us
    all_to_all x1, waiting for transfers between devices, route(): lax.all_to_all(slot_array, 'rev', split_axis=0, concat_axis=0, tiled=True)  26.4 us
    dot_general x20, matrix products, mixing(): return jnp.einsum('bio,bipq->bopq', matrix, values, precision=HIGHEST)  25.2 us
    unnamed x51, local copies, waits for them, and re-layouts  22.5 us
    all_to_all x1, waiting for transfers between devices, local(): lax.all_to_all(grad_cols, 'row', split_axis=3, concat_axis=2, tiled=True)  21.7 us
    dot_general x2, matrix products, column_pass(): imag_cols = -jnp.dot(flattened, col_sin, preferred_element_type=jnp.float32)  16.1 us
  transfers between devices with their start and end apart: 4, of which 3 were waited for; matrix products, arithmetic and copies ran while one was open for 18% of the time, Pallas kernels for 0%

commit v1 on v0

v1 whole, which is shorter than its diff:
```python
import functools
import math

import jax
import jax.numpy as jnp
import ml_dtypes
import numpy as np
from jax import lax
from jax.experimental import pallas as pl
from jax.experimental.pallas import tpu as pltpu
from jax.sharding import PartitionSpec as P

KX = 128
MB = 16
KY = 256
BF16 = jnp.bfloat16
F32 = jnp.float32
GELU_A = math.sqrt(2.0 / math.pi)
GELU_B = 0.044715


def column_tables(n_cols):
    phases = np.arange(n_cols)[:, None] * np.arange(KX)[None, :] % n_cols
    angles = phases.astype(np.float32) * np.float32(2.0 * math.pi / n_cols)
    both = np.concatenate([np.cos(angles), -np.sin(angles)], axis=1)
    return both.astype(ml_dtypes.bfloat16)


def row_tables(n_rows, shards):
    slot = np.arange(KY)
    signed = np.where(slot < KY // 2, slot, slot - KY + n_rows)
    phases = signed[:, None] * np.arange(n_rows)[None, :] % n_rows
    angles = phases.astype(np.float32) * np.float32(2.0 * math.pi / n_rows)
    both = np.concatenate([np.cos(angles), np.sin(angles)], axis=0)
    split = both.reshape(2 * KY, shards, n_rows // shards).transpose(1, 0, 2)
    return np.ascontiguousarray(split).astype(ml_dtypes.bfloat16)


def forward_kernel(channels, scale, x_ref, col_ref, row_ref, out_ref, held):
    step = pl.program_id(0)
    cols = jnp.dot(x_ref[0], col_ref[...], preferred_element_type=F32).astype(BF16)
    quads = jnp.dot(row_ref[...], cols, preferred_element_type=F32)
    real = (quads[:KY, :KX] + quads[KY:, KX:]) * scale
    imag = (quads[:KY, KX:] - quads[KY:, :KX]) * scale
    held[pl.ds(pl.multiple_of(step * KY, KY), KY), :] = real
    held[pl.ds(pl.multiple_of((channels + step) * KY, KY), KY), :] = imag

    @pl.when(step == channels - 1)
    def _():
        def turn(j, carry):
            out_ref[j] = held[pl.ds(j, 2 * channels, stride=KY), :].astype(BF16)
            return carry

        lax.fori_loop(0, KY, turn, 0, unroll=8)


def forward_partial(field, col_table, row_table, scale):
    channels, n_rows, n_cols = field.shape
    return pl.pallas_call(
        functools.partial(forward_kernel, channels, scale),
        grid=(channels,),
        out_shape=jax.ShapeDtypeStruct((KY, 2 * channels, KX), BF16),
        in_specs=[
            pl.BlockSpec((1, n_rows, n_cols), lambda c: (c, 0, 0)),
            pl.BlockSpec((n_cols, 2 * KX), lambda c: (0, 0)),
            pl.BlockSpec((2 * KY, n_rows), lambda c: (0, 0)),
        ],
        out_specs=pl.BlockSpec((KY, 2 * channels, KX), lambda c: (0, 0, 0)),
        scratch_shapes=[pltpu.VMEM((2 * channels * KY, KX), F32)],
        compiler_params=pltpu.CompilerParams(
            dimension_semantics=("arbitrary",), vmem_limit_bytes=32 << 20
        ),
        cost_estimate=pl.CostEstimate(
            flops=channels * n_rows * 2 * KX * (2 * n_cols + 4 * KY),
            bytes_accessed=2 * field.size + 4 * KY * channels * KX,
            transcendentals=0,
        ),
    )(field, col_table, row_table)


def inverse_kernel(channels, scale, total_ref, row_ref, col_ref, out_ref, held):
    step = pl.program_id(0)

    @pl.when(step == 0)
    def _():
        def turn(j, carry):
            at = pl.multiple_of(j * 2 * channels, 2 * channels)
            held[pl.ds(at, 2 * channels), :] = total_ref[j].astype(F32)
            return carry

        lax.fori_loop(0, KY, turn, 0, unroll=8)

    real = held[pl.ds(step, KY, stride=2 * channels), :].astype(BF16)
    imag = held[pl.ds(channels + step, KY, stride=2 * channels), :].astype(BF16)
    pair = jnp.concatenate([real, imag], axis=1)
    n_rows = out_ref.shape[1]
    quads = lax.dot_general(
        row_ref[...], pair, (((1,), (0,)), ((), ())), preferred_element_type=F32
    )
    rows_re = quads[:n_rows, :KX] - quads[n_rows:, KX:]
    rows_im = quads[n_rows:, :KX] + quads[:n_rows, KX:]
    rows = jnp.concatenate([rows_re, rows_im], axis=1).astype(BF16)
    field = jnp.dot(rows, col_ref[...], preferred_element_type=F32) * scale
    out_ref[0] = field.astype(BF16)


def inverse_field(total, row_table_t, col_table_t, scale):
    channels = total.shape[1] // 2
    n_rows, n_cols = row_table_t.shape[0] // 2, col_table_t.shape[1]
    return pl.pallas_call(
        functools.partial(inverse_kernel, channels, scale),
        grid=(channels,),
        out_shape=jax.ShapeDtypeStruct((channels, n_rows, n_cols), BF16),
        in_specs=[
            pl.BlockSpec((KY, 2 * channels, KX), lambda c: (0, 0, 0)),
            pl.BlockSpec((2 * n_rows, KY), lambda c: (0, 0)),
            pl.BlockSpec((2 * KX, n_cols), lambda c: (0, 0)),
        ],
        out_specs=pl.BlockSpec((1, n_rows, n_cols), lambda c: (c, 0, 0)),
        scratch_shapes=[pltpu.VMEM((2 * channels * KY, KX), F32)],
        compiler_params=pltpu.CompilerParams(
            dimension_semantics=("arbitrary",), vmem_limit_bytes=32 << 20
        ),
        cost_estimate=pl.CostEstimate(
            flops=channels * n_rows * 2 * KX * (2 * n_cols + 4 * KY),
            bytes_accessed=2 * channels * n_rows * n_cols + 4 * KY * channels * KX,
            transcendentals=0,
        ),
    )(total, row_table_t, col_table_t)


def mlp_kernel(
    slots, group, width, slot0_ref, kept_ref, own_ref, other_ref, cot_ref, win_ref, bias_ref,
    wout_t_ref, win_t_ref, own_out, other_out, sums_ref,
):
    step = pl.program_id(0)

    @pl.when(step == 0)
    def _():
        sums_ref[...] = jnp.zeros_like(sums_ref)

    lanes = lax.broadcasted_iota(jnp.int32, (width, KX), 1)
    limit = kept_ref[0] * MB
    own, other, cot = [], [], []
    for g in range(group):
        slot = slot0_ref[0] + step * group + g
        extent = jnp.where(slot < KY // 2, slot, KY - slot)
        keep = jnp.maximum(lanes, extent) < limit
        own.append(own_ref[g])
        other.append(other_ref[g])
        cot.append(jnp.where(keep, cot_ref[g].astype(F32), 0.0).astype(BF16))
    joined = jnp.concatenate(
        [jnp.concatenate(own, axis=1), jnp.concatenate(other, axis=1)], axis=0
    )
    cotangent = jnp.concatenate(cot, axis=1)

    def times(weights, values):
        parts = jnp.dot(weights, values, preferred_element_type=F32)
        half = parts.shape[0] // 2
        return parts[:half] + parts[half:]

    pre = times(win_ref[...], joined) + bias_ref[:, 0:1]
    square = pre * pre
    bend = jnp.tanh(GELU_A * (pre + GELU_B * (square * pre)))
    hidden = 0.5 * pre * (1.0 + bend)
    slope = 0.5 * (1.0 + bend) + 0.5 * pre * (1.0 - bend * bend) * (
        GELU_A * (1.0 + (3.0 * GELU_B) * square)
    )
    grad_pre = (times(wout_t_ref[...], cotangent) * slope).astype(BF16)
    grad_joined = times(win_t_ref[...], grad_pre)
    for g in range(group):
        at = slice(g * KX, (g + 1) * KX)
        own_out[g] = grad_joined[:width, at].astype(BF16)
        other_out[g] = grad_joined[width:, at].astype(BF16)
    left = jnp.concatenate([grad_pre, cotangent], axis=0)
    ones = jnp.ones((width, group * KX), BF16)
    right = jnp.concatenate([joined, hidden.astype(BF16), ones], axis=0)
    sums_ref[...] += lax.dot_general(
        left, right, (((1,), (1,)), ((), ())), preferred_element_type=F32
    )


def mlp(slot0, kept, own, other, cot, win, bias, wout_t, win_t):
    slots, width, _ = own.shape
    group = 8
    while slots % group:
        group //= 2
    block = pl.BlockSpec((group, width, KX), lambda i: (i, 0, 0))
    scalar = pl.BlockSpec(memory_space=pltpu.SMEM)

    def whole(array):
        return pl.BlockSpec(array.shape, lambda i: (0, 0))

    return pl.pallas_call(
        functools.partial(mlp_kernel, slots, group, width),
        grid=(slots // group,),
        out_shape=(
            jax.ShapeDtypeStruct(own.shape, BF16),
            jax.ShapeDtypeStruct(own.shape, BF16),
            jax.ShapeDtypeStruct((2 * width, 4 * width), F32),
        ),
        in_specs=[
            scalar, scalar, block, block, block, whole(win), whole(bias), whole(wout_t), whole(win_t),
        ],
        out_specs=(block, block, pl.BlockSpec((2 * width, 4 * width), lambda i: (0, 0))),
        compiler_params=pltpu.CompilerParams(
            dimension_semantics=("arbitrary",), vmem_limit_bytes=32 << 20
        ),
        cost_estimate=pl.CostEstimate(
            flops=slots * KX * 2 * width * 16 * width,
            bytes_accessed=10 * own.size,
            transcendentals=slots * KX * width,
        ),
    )(slot0, kept, own, other, cot, win, bias, wout_t, win_t)


def split_rows(matrix):
    high = matrix.astype(BF16)
    low = (matrix - high.astype(F32)).astype(BF16)
    return jnp.concatenate([high, low], axis=0)


def block_matrix(blocks):
    count, m, n = blocks.shape
    if count == 1:
        return blocks[0]
    eye = jnp.eye(count, dtype=F32)
    return (blocks[:, :, None, :] * eye[:, None, :, None]).reshape(count * m, count * n)


def block_parts(matrix, count):
    rows, cols = matrix.shape
    split = matrix.reshape(count, rows // count, count, cols // count)
    return jnp.stack([split[b, :, b, :] for b in range(count)])


def local(fields, out_grads, partner, kept_blocks, weight_in, bias_in, weight_out):
    shards = lax.axis_size("row")
    channels, rows, n_cols = fields.shape[1:]
    n_rows = rows * shards
    count, bs = weight_out.shape[0], weight_out.shape[-1]
    own_rev = lax.axis_index("rev")
    row_rank = lax.axis_index("row")
    slots = KY // shards
    scale = 1.0 / math.sqrt(n_rows * n_cols)
    col_np = column_tables(n_cols)
    row_np = row_tables(n_rows, shards)
    col_table = jnp.asarray(col_np)
    row_table = lax.dynamic_index_in_dim(jnp.asarray(row_np), row_rank, 0, keepdims=False)
    inv_np = row_np.reshape(shards, 2, KY, rows).transpose(0, 1, 3, 2).reshape(shards, 2 * rows, KY)
    inv_table = lax.dynamic_index_in_dim(
        jnp.asarray(np.ascontiguousarray(inv_np)), row_rank, 0, keepdims=False
    )

    def spectrum(field):
        part = forward_partial(field, col_table, row_table, scale)
        return lax.psum_scatter(part, "row", scatter_dimension=0, tiled=True)

    spectra = spectrum(fields[0])
    grad_spec = spectrum(out_grads[0])
    target = partner[own_rev]

    def route(values):
        every = lax.all_gather(values, "rev", axis=0, tiled=False)
        return lax.dynamic_index_in_dim(every, target, 0, keepdims=False)

    own_real = block_matrix(weight_in[:, 0, :bs])
    own_imag = block_matrix(weight_in[:, 1, :bs])
    other_real = block_matrix(weight_in[:, 0, bs:])
    other_imag = block_matrix(weight_in[:, 1, bs:])
    out_real = block_matrix(weight_out[:, 0])
    out_imag = block_matrix(weight_out[:, 1])
    win_t = jnp.concatenate(
        [
            jnp.concatenate([own_real, own_imag], axis=1),
            jnp.concatenate([-own_imag, own_real], axis=1),
            jnp.concatenate([other_real, other_imag], axis=1),
            jnp.concatenate([-other_imag, other_real], axis=1),
        ],
        axis=0,
    )
    wout_t = jnp.concatenate(
        [
            jnp.concatenate([out_real, out_imag], axis=1),
            jnp.concatenate([-out_imag, out_real], axis=1),
        ],
        axis=0,
    )
    bias = jnp.concatenate([bias_in[:, 0].reshape(-1), bias_in[:, 1].reshape(-1)])
    bias = jnp.broadcast_to(bias[:, None], (2 * channels, KX))
    own_grads, other_grads, sums = mlp(
        (row_rank * slots).reshape(1).astype(jnp.int32),
        kept_blocks[own_rev].reshape(1),
        spectra,
        route(spectra),
        grad_spec,
        split_rows(win_t.T),
        bias,
        split_rows(wout_t),
        split_rows(win_t),
    )
    returned = route(other_grads)
    total = (own_grads.astype(F32) + returned.astype(F32)).astype(BF16)
    gathered = lax.all_gather(total, "row", axis=0, tiled=True)
    field_grads = inverse_field(gathered, inv_table, col_table.T, scale)

    summed = lax.psum(sums, ("rev", "row")) * (1.0 / math.sqrt(lax.axis_size("rev") * KX * KY))
    width = 2 * channels
    pre, cot = summed[:width], summed[width:]

    def complex_parts(grad):
        top, bottom = grad[:channels], grad[channels:]
        real = top[:, :channels] + bottom[:, channels:]
        imag = bottom[:, :channels] - top[:, channels:]
        return jnp.stack([block_parts(real.T, count), block_parts(imag.T, count)], axis=1)

    grad_win = jnp.concatenate(
        [complex_parts(pre[:, :width]), complex_parts(pre[:, width : 2 * width])], axis=2
    )
    grad_wout = complex_parts(cot[:, 2 * width : 3 * width])

    def bias_parts(column):
        return column.reshape(2, count, bs).transpose(1, 0, 2)

    return (
        field_grads[None],
        grad_win,
        bias_parts(pre[:, 3 * width]),
        grad_wout,
        bias_parts(cot[:, 3 * width]),
    )


def solution(mesh):
    placed = (P("rev", None, "row", None), P("rev", None, "row", None), P(), P(), P(), P(), P())
    return jax.shard_map(
        local,
        mesh=mesh,
        in_specs=placed,
        out_specs=(P("rev", None, "row", None), P(), P(), P(), P()),
        check_vma=False,
    )
```

time: 393 us -> 271 us (0.69); the launches traced: 385 us -> 271 us
  matrix products: 93.7 us -> 0 us
  waiting for transfers between devices: 78.3 us -> 146 us
  blocking collectives: 109 us -> 42.4 us
  local copies, waits for them, and re-layouts: 65.6 us -> 17.1 us
  Pallas kernels: 0 us -> 45.6 us
  starting transfers between devices: 19.5 us -> 0.2 us
  between operations: 4.32 us -> 15.9 us
  other arithmetic: 14.8 us -> 3.26 us
    dot_general x32 -> x0, matrix products: 93.7 us -> none  [the longest x20 25.2 us: mixing(): return jnp.einsum('bio,bipq->bopq', matrix, values, precision=HIGHEST)]
    reduce_scatter x0 -> x2, waiting for transfers between devices: none -> 92.5 us  [spectrum(): return lax.psum_scatter(part, 'row', scatter_dimension=0, tiled=True)]
    all_to_all x4 -> x0, waiting for transfers between devices: 78.3 us -> none  [the longest x1 30.2 us: local(): lax.all_to_all(field_cols, 'row', split_axis=3, concat_axis=2, tiled=True)]
    all_gather x0 -> x3, waiting for transfers between devices: none -> 53.8 us  [the longest x2 53 us: route(): every = lax.all_gather(values, 'rev', axis=0, tiled=False)]
    all_to_all x1 -> x0, blocking collectives: 51.6 us -> none  [route(): lax.all_to_all(slot_array, 'rev', split_axis=0, concat_axis=0, tiled=True)]
    pallas_call x0 -> x4, Pallas kernels: none -> 45.6 us  [the longest x2 27.5 us: forward_partial(): pl.pallas_call(functools.partial(forward_kernel, channels, scale), grid=(...]
    all_to_all x5 -> x0, local copies, waits for them, and re-layouts: 26.3 us -> none  [the longest x1 10.9 us: local(): lax.all_to_all(rows_spec, 'row', split_axis=2, concat_axis=3, tiled=True)]
    all_to_all x4 -> x0, starting transfers between devices: 19.5 us -> none  [the longest x1 6.52 us: local(): lax.all_to_all(field_cols, 'row', split_axis=3, concat_axis=2, tiled=True)]
  transfers between devices with their start and end apart: 4 -> 5, of which waited for: 3 -> 5; matrix products, arithmetic and copies ran while one was open for 18% -> 3% of each run, Pallas kernels for 0% -> 5%
where the time goes in v1:
time: 271 us
  waiting for transfers between devices  146 us (54%)
  Pallas kernels  45.6 us (17%)
  blocking collectives  42.4 us (16%)
  local copies, waits for them, and re-layouts  17.1 us (6%)
  between operations  15.9 us (6%)
  other arithmetic  3.26 us (1%)
    reduce_scatter x2, waiting for transfers between devices, spectrum(): return lax.psum_scatter(part, 'row', scatter_dimension=0, tiled=True)  92.5 us
    all_gather x2, waiting for transfers between devices, route(): every = lax.all_gather(values, 'rev', axis=0, tiled=False)  53 us
    psum x1, blocking collectives, local(): lax.psum(sums, ('rev', 'row'))  42.4 us
    pallas_call x2, Pallas kernels, forward_partial(): pl.pallas_call(functools.partial(forward_kernel, channels, scale), grid=(...  27.5 us
    pallas_call x1, Pallas kernels, inverse_field(): pl.pallas_call(functools.partial(inverse_kernel, channels, scale), grid=(...  12.7 us
    unnamed x27, local copies, waits for them, and re-layouts  11.1 us
  transfers between devices with their start and end apart: 5, of which 5 were waited for; matrix products, arithmetic and copies ran while one was open for 3% of the time, Pallas kernels for 5%

profile of v1, /device:TPU:0, one launch (start us, length us, event | category | flops | bytes accessed | tf_op | source)
XLA Modules:
  0.0 270.7 jit_solution(1624933315491501306)
XLA Ops:
  7.2 0.0 reduce-scatter.3.cloned.1.call-start
  7.2 1.0 dynamic-slice_bitcast_fusion.2.row_ref
  8.2 3.4 %copy-done.2 = bf16[1,16,256,1024]{3,2,1,0:T(8,128)(2,1)S(1)} copy-done((bf16[1,16,256,1024]{3,2,1,0:T(8,128)(2,1)S(1)}, bf16[1,16,256,1024]{3,2,1,0:T(8,128)(2,1)}, u32[]{:S(2)}) %copy-start.2) | copy-done | bytes 8388632
  11.6 1.0 copy-done.6
  12.6 13.7 %shard_map.137 = bf16[256,32,128]{2,1,0:T(8,128)(2,1)} custom-call(bf16[16,256,1024]{2,1,0:T(8,128)(2,1)S(1)} %bitcast.68, bf16[1024,256]{1,0:T(8,128)(2,1)S(1)} %copy-done.6, bf16[512,256]{1,0:T(8,128)(2,1)S(1)} %dynamic-slice_bitcast_fusion.2.row_ref), custom_call_target="tpu_custom_call" | custom-call | flops 3221225472 | bytes 10485760 | tf_op jit(solution)/shard_map/pallas_call | solution.py:59
  26.4 0.0 reduce-scatter.3.cloned.1.call-update
  26.4 0.0 all-gather.8.cloned.1.call-start
  26.4 46.7 %reduce-scatter.3.cloned.1.call-done.own_ref = bf16[64,32,128]{2,1,0:T(8,128)(2,1)} async-done(((bf16[256,32,128]{2,1,0:T(8,128)(2,1)}), bf16[64,32,128]{2,1,0:T(8,128)(2,1)}) %reduce-scatter.3.cloned.1.call-update) | async-done | bytes 524304 | tf_op jit(solution)/shard_map/reduce_scatter | solution.py:257
  73.1 0.0 all-gather.8.cloned.1.call-update
  73.1 0.0 reduce-scatter.5.cloned.1.call-start
  73.2 0.0 copy-start.3
  73.2 3.4 %copy-done.3 = bf16[1,16,256,1024]{3,2,1,0:T(8,128)(2,1)S(1)} copy-done((bf16[1,16,256,1024]{3,2,1,0:T(8,128)(2,1)S(1)}, bf16[1,16,256,1024]{3,2,1,0:T(8,128)(2,1)}, u32[]{:S(2)}) %copy-start.3) | copy-done | bytes 8388632
  76.6 0.0 copy-start.9
  76.6 13.8 %shard_map.138 = bf16[256,32,128]{2,1,0:T(8,128)(2,1)} custom-call(bf16[16,256,1024]{2,1,0:T(8,128)(2,1)S(1)} %bitcast.69, bf16[1024,256]{1,0:T(8,128)(2,1)S(1)} %copy-done.7, bf16[512,256]{1,0:T(8,128)(2,1)S(1)} %dynamic-slice_bitcast_fusion.2.row_ref), custom_call_target="tpu_custom_call" | custom-call | flops 3221225472 | bytes 10485760 | tf_op jit(solution)/shard_map/pallas_call | solution.py:59
  90.4 0.0 reduce-scatter.5.cloned.1.call-update
  90.4 0.0 all-gather.10.cloned.1.call-start
  90.4 0.6 dynamic_slice.22
  92.3 0.6 dynamic_slice.20.kept_ref
  92.9 0.1 fusion.9
  93.0 0.1 slice_bitcast_fusion.4
  93.1 0.1 subtract_convert_fusion
  93.2 0.1 pad_maximum_fusion.3
  93.3 0.1 copy.27.win_t_ref
  94.1 0.1 pad_maximum_fusion.4
  94.1 0.1 subtract_convert_fusion.1
  94.2 0.1 fusion.8
  94.3 16.9 %all-gather.8.cloned.1.call-done = bf16[512,32,128]{2,1,0:T(8,128)(2,1)} async-done(((bf16[64,32,128]{2,1,0:T(8,128)(2,1)}), bf16[512,32,128]{2,1,0:T(8,128)(2,1)}) %all-gather.8.cloned.1.call-update) | async-done | bytes 4194320 | tf_op jit(solution)/shard_map/all_gather | solution.py:264
  111.2 1.1 dynamic-slice_bitcast_fusion.other_ref
  112.3 45.8 %reduce-scatter.5.cloned.1.call-done.cot_ref = bf16[64,32,128]{2,1,0:T(8,128)(2,1)} async-done(((bf16[256,32,128]{2,1,0:T(8,128)(2,1)}), bf16[64,32,128]{2,1,0:T(8,128)(2,1)}) %reduce-scatter.5.cloned.1.call-update) | async-done | bytes 524304 | tf_op jit(solution)/shard_map/reduce_scatter | solution.py:257
  158.1 0.1 broadcast_in_dim.4.bias_ref
  158.2 1.0 copy-done.1
  159.2 5.3 %shard_map.139 = (bf16[64,32,128]{2,1,0:T(8,128)(2,1)S(1)}, bf16[64,32,128]{2,1,0:T(8,128)(2,1)}, f32[64,128]{1,0:T(8,128)S(1)}) custom-call(s32[1]{0:T(128)} %bitcast.slot0_ref, s32[1]{0:T(128)} %dynamic_slice.20.kept_ref, bf16[64,32,128]{2,1,0:T(8,128)(2,1)S(1)} %copy-done, bf16[64,32,128]{2,1,0:T(8,128)(2,1)S(1)} %dynamic-slice_bitcast_fusion.other_ref, ...), custom_call_target="tpu_custom_call" | custom-call | flops 268435456 | bytes 2621440 | tf_op jit(solution)/shard_map/pallas_call | solution.py:194
  164.6 0.0 all-gather.10.cloned.1.call-update
  164.6 0.0 all-gather.6.cloned.1.call-start
  164.6 36.1 %all-gather.10.cloned.1.call-done = bf16[512,32,128]{2,1,0:T(8,128)(2,1)} async-done(((bf16[64,32,128]{2,1,0:T(8,128)(2,1)}), bf16[512,32,128]{2,1,0:T(8,128)(2,1)}) %all-gather.10.cloned.1.call-update) | async-done | bytes 4194320 | tf_op jit(solution)/shard_map/all_gather | solution.py:264
  200.8 2.0 fusion
  202.7 0.0 all-gather.6.cloned.1.call-update
  202.8 1.0 dynamic-slice_bitcast_fusion.1.row_ref
  203.7 42.4 %psum.7 = f32[64,128]{1,0:T(8,128)S(1)} all-reduce(f32[64,128]{1,0:T(8,128)S(1)} %get-tuple-element.10), channel_id=1, replica_groups=mesh['rev'=8,'row'=4] {'rev','row'}, use_global_device_ids=true, to_apply=%region_2.3 | all-reduce | flops 8192 | bytes 65536 | tf_op jit(solution)/shard_map/psum | solution.py:307
  246.1 0.2 slice_reduce_fusion
  246.3 0.7 transpose_reshape_squeeze.6
  247.0 0.1 fusion.3
  247.1 0.7 copy.28
  247.7 0.6 transpose_reshape_squeeze.7
  248.4 0.7 maximum_maximum_fusion.2
  249.1 0.8 all-gather.6.cloned.1.call-done.total_ref
  249.9 1.6 copy-done.4
  251.4 12.7 %shard_map.140 = bf16[16,256,1024]{2,1,0:T(8,128)(2,1)} custom-call(bf16[256,32,128]{2,1,0:T(8,128)(2,1)S(1)} %copy-done.4, bf16[512,256]{1,0:T(8,128)(2,1)S(1)} %dynamic-slice_bitcast_fusion.1.row_ref, bf16[256,1024]{1,0:T(8,128)(2,1)S(1)} %copy-done.5), custom_call_target="tpu_custom_call" | custom-call | flops 3221225472 | bytes 10485760 | tf_op jit(solution)/shard_map/pallas_call | solution.py:110
  (27 shorter events, 0.1 us)
Async XLA Ops:
  7.2 65.9 %reduce-scatter.3.cloned.1.call-start = ((), (), s32[]{:S(2)}) async-start(), calls=%async_computation.2 | async-start | bytes 2621440 | tf_op jit(solution)/shard_map/reduce_scatter | solution.py:257
  8.2 3.4 %copy-start.2 = (bf16[1,16,256,1024]{3,2,1,0:T(8,128)(2,1)S(1)}, bf16[1,16,256,1024]{3,2,1,0:T(8,128)(2,1)}, u32[]{:S(2)}) copy-start(bf16[1,16,256,1024]{3,2,1,0:T(8,128)(2,1)} %param.10) | copy-start | bytes 25165828
  11.6 1.0 copy-start.6
  12.6 60.6 %copy-start.7 = (bf16[1024,256]{1,0:T(8,128)(2,1)S(1)}, bf16[1024,256]{1,0:T(8,128)(2,1)}, u32[]{:S(2)}) copy-start(bf16[1024,256]{1,0:T(8,128)(2,1)} %constant.36.clone.col_ref) | copy-start | bytes 1572868
  26.4 84.8 %all-gather.8.cloned.1.call-start = ((), (), s32[]{:S(2)}) async-start(), calls=%async_computation.5 | async-start | bytes 4718592 | tf_op jit(solution)/shard_map/all_gather | solution.py:264
  73.1 85.0 %reduce-scatter.5.cloned.1.call-start = ((), (), s32[]{:S(2)}) async-start(), calls=%async_computation.3 | async-start | bytes 2621440 | tf_op jit(solution)/shard_map/reduce_scatter | solution.py:257
  73.2 3.4 %copy-start.3 = (bf16[1,16,256,1024]{3,2,1,0:T(8,128)(2,1)S(1)}, bf16[1,16,256,1024]{3,2,1,0:T(8,128)(2,1)}, u32[]{:S(2)}) copy-start(bf16[1,16,256,1024]{3,2,1,0:T(8,128)(2,1)} %param.11) | copy-start | bytes 25165828
  76.6 13.9 %copy-start.11 = (s32[8]{0:T(128)S(1)}, s32[8]{0:T(128)}, u32[]{:S(2)}) copy-start(s32[8]{0:T(128)} %param.12) | copy-start | bytes 100
  76.6 15.8 %copy-start.12 = (s32[8]{0:T(128)S(1)}, s32[8]{0:T(128)}, u32[]{:S(2)}) copy-start(s32[8]{0:T(128)} %param.13) | copy-start | bytes 100
  76.6 16.4 %copy-start.8 = (f32[1,2,32,16]{2,3,1,0:T(8,128)S(1)}, f32[1,2,32,16]{2,3,1,0:T(8,128)}, u32[]{:S(2)}) copy-start(f32[1,2,32,16]{2,3,1,0:T(8,128)} %param.14) | copy-start | bytes 12292
  76.6 17.5 %copy-start.10 = (f32[1,2,16]{2,1,0:T(2,128)S(1)}, f32[1,2,16]{2,1,0:T(2,128)}, u32[]{:S(2)}) copy-start(f32[1,2,16]{2,1,0:T(2,128)} %param.15) | copy-start | bytes 388
  76.6 17.6 %copy-start.9 = (f32[1,2,16,16]{3,2,1,0:T(8,128)S(1)}, f32[1,2,16,16]{3,2,1,0:T(8,128)}, u32[]{:S(2)}) copy-start(f32[1,2,16,16]{3,2,1,0:T(8,128)} %param.16) | copy-start | bytes 6148
  76.6 81.6 %copy-start = (bf16[64,32,128]{2,1,0:T(8,128)(2,1)S(1)}, bf16[64,32,128]{2,1,0:T(8,128)(2,1)}, u32[]{:S(2)}) copy-start(bf16[64,32,128]{2,1,0:T(8,128)(2,1)} %reduce-scatter.3.cloned.1.call-done.own_ref) | copy-start | bytes 1572868
  90.4 159.5 %copy-start.5 = (bf16[256,1024]{1,0:T(8,128)(2,1)S(1)}, bf16[256,1024]{1,0:T(8,128)(2,1)}, u32[]{:S(2)}) copy-start(bf16[256,1024]{1,0:T(8,128)(2,1)} %constant.41.col_ref) | copy-start | bytes 1572868
  90.4 110.4 %all-gather.10.cloned.1.call-start = ((), (), s32[]{:S(2)}) async-start(), calls=%async_computation.6 | async-start | bytes 4718592 | tf_op jit(solution)/shard_map/all_gather | solution.py:264
  158.2 1.0 copy-start.1
  164.6 85.3 %all-gather.6.cloned.1.call-start = ((), (), s32[]{:S(2)}) async-start(), calls=%async_computation.4 | async-start | bytes 2621440 | tf_op jit(solution)/shard_map/all_gather | solution.py:304
  249.9 1.6 copy-start.4
Sparse Core Ops, SparseCore 0:
  26.5 46.5 reduce-scatter.2
  75.2 36.0 all-gather.7
  114.2 43.8 reduce-scatter.4
  164.7 36.0 all-gather.9
  202.9 46.9 all-gather.5

commit v2 on v1

--- a/solution.py
+++ b/solution.py
@@ -214,6 +214,326 @@
     )(slot0, kept, own, other, cot, win, bias, wout_t, win_t)
 
 
+MESH = pl.DeviceIdType.MESH
+
+
+class Line:
+    def __init__(self, size, send_sems, recv_sems):
+        self.size, self.send_sems, self.recv_sems = size, send_sems, recv_sems
+        self.me = lax.axis_index("row")
+
+    def copy(self, side, tag, source, target):
+        return pltpu.make_async_remote_copy(
+            src_ref=source,
+            dst_ref=target,
+            send_sem=self.send_sems.at[side, tag],
+            recv_sem=self.recv_sems.at[side, tag],
+            device_id={"row": self.me + 1 - 2 * side},
+            device_id_type=MESH,
+        )
+
+
+class Cube:
+    def __init__(self, slots, send_sems, recv_sems):
+        self.slots, self.send_sems, self.recv_sems = slots, send_sems, recv_sems
+        self.me = lax.axis_index("rev")
+        core, x, y = self.me % 2, (self.me // 2) % 2, self.me // 4
+        self.step = {"c": 1 - 2 * core, "x": 2 - 4 * x, "y": 4 - 8 * y}
+
+    def copy(self, tag, axis, slot, part=None):
+        block = self.slots.at[slot]
+        if part is not None:
+            half = self.slots.shape[1] // 2
+            block = self.slots.at[slot, pl.ds(part * half, half)]
+        return pltpu.make_async_remote_copy(
+            src_ref=block,
+            dst_ref=block,
+            send_sem=self.send_sems.at[tag],
+            recv_sem=self.recv_sems.at[tag],
+            device_id={"rev": self.me + self.step[axis]},
+            device_id_type=MESH,
+        )
+
+    def numbered(self, tag):
+        me, step = self.me, self.step
+        axis, slot, part = (
+            ("x", me, None),
+            ("y", me, None),
+            ("c", me, None),
+            ("y", me + step["x"], 0),
+            ("x", me + step["y"], 1),
+            ("c", me + step["x"], None),
+            ("c", me + step["y"], None),
+            ("c", me + step["x"] + step["y"], None),
+        )[tag]
+        return self.copy(tag, axis, slot, part)
+
+    def received(self, *tags):
+        for tag in tags:
+            self.numbered(tag).wait_recv()
+
+    def start(self, *tags):
+        for tag in tags:
+            self.numbered(tag).start()
+
+    def first(self):
+        self.start(0, 1, 2)
+
+    def second(self):
+        self.received(0, 1)
+        self.start(3, 4, 5, 6)
+
+    def third(self):
+        self.received(3, 4)
+        self.start(7)
+
+    def last(self):
+        self.received(2, 5, 6, 7)
+        for tag in range(8):
+            self.numbered(tag).wait_send()
+
+
+def greet(size, with_cube):
+    me = lax.axis_index("row")
+    barrier = pltpu.get_barrier_semaphore()
+    sides = ((me < size - 1, me + 1), (me > 0, me - 1))
+    for there, neighbour in sides:
+
+        @pl.when(there)
+        def _(neighbour=neighbour):
+            pl.semaphore_signal(
+                barrier, inc=1, device_id={"row": neighbour}, device_id_type=MESH
+            )
+
+    if with_cube:
+        rev = lax.axis_index("rev")
+        core, x, y = rev % 2, (rev // 2) % 2, rev // 4
+        for other in (rev + 1 - 2 * core, rev + 2 - 4 * x, rev + 4 - 8 * y):
+            pl.semaphore_signal(barrier, inc=1, device_id={"rev": other}, device_id_type=MESH)
+
+    at_end = (me == 0) | (me == size - 1)
+    around = 3 if with_cube else 0
+
+    @pl.when(at_end)
+    def _():
+        pl.semaphore_wait(barrier, around + 1)
+
+    @pl.when(jnp.logical_not(at_end))
+    def _():
+        pl.semaphore_wait(barrier, around + 2)
+
+
+def add_into(held, side, slot, part_ref):
+    held[side, slot] = (held[side, slot].astype(F32) + part_ref[slot].astype(F32)).astype(BF16)
+
+
+def reduce_step(line, held, base, part_ref, t):
+    n, me = line.size, line.me
+    for side in (0, 1):
+        place = me if side == 0 else n - 1 - me
+        slot = n - 1 - t + me if side == 0 else t - (n - 1 - me)
+        ahead = 1 if side == 0 else -1
+
+        @pl.when((place <= t) & (place < n - 1))
+        def _(side=side, place=place, slot=slot, ahead=ahead):
+            copy = line.copy(side, base + slot, held.at[side, slot], held.at[side, slot])
+
+            @pl.when(place > 0)
+            def _():
+                copy.wait_recv()
+                add_into(held, side, slot, part_ref)
+
+            @pl.when(place == 0)
+            def _():
+                held[side, slot] = part_ref[slot]
+
+            @pl.when(place < t)
+            def _():
+                old = slot + ahead
+                line.copy(side, base + old, held.at[side, old], held.at[side, old]).wait_send()
+
+            copy.start()
+
+
+def reduce_last(line, held, base, part_ref, out_ref):
+    n, me = line.size, line.me
+    for side in (0, 1):
+        place = me if side == 0 else n - 1 - me
+        ahead = 1 if side == 0 else -1
+
+        @pl.when(place > 0)
+        def _(side=side):
+            line.copy(side, base + me, held.at[side, me], held.at[side, me]).wait_recv()
+
+    @pl.when((me > 0) & (me < n - 1))
+    def _():
+        total = part_ref[me].astype(F32) + held[0, me].astype(F32) + held[1, me].astype(F32)
+        out_ref[...] = total.astype(BF16)
+
+    @pl.when(me == 0)
+    def _():
+        out_ref[...] = (part_ref[me].astype(F32) + held[1, me].astype(F32)).astype(BF16)
+
+    @pl.when(me == n - 1)
+    def _():
+        out_ref[...] = (part_ref[me].astype(F32) + held[0, me].astype(F32)).astype(BF16)
+
+
+def reduce_sent(line, held, base):
+    n, me = line.size, line.me
+    for side in (0, 1):
+        place = me if side == 0 else n - 1 - me
+        slot = me + 1 if side == 0 else me - 1
+
+        @pl.when(place < n - 1)
+        def _(side=side, slot=slot):
+            line.copy(side, base + slot, held.at[side, slot], held.at[side, slot]).wait_send()
+
+
+def exchange_kernel(
+    n, revs, partner_ref, part_f, part_g, own_ref, other_ref, cot_ref, held_f, held_g, slots,
+    line_send, line_recv, cube_send, cube_recv,
+):
+    greet(n, True)
+    line = Line(n, line_send, line_recv)
+    cube = Cube(slots, cube_send, cube_recv)
+    for t in range(n - 1):
+        reduce_step(line, held_f, 0, part_f, t)
+    reduce_last(line, held_f, 0, part_f, own_ref)
+    slots[cube.me] = own_ref[...]
+    cube.first()
+    reduce_sent(line, held_f, 0)
+    for t in range(n - 1):
+        reduce_step(line, held_g, n, part_g, t)
+        if t == 0:
+            cube.second()
+        if t == 1:
+            cube.third()
+    if n < 3:
+        cube.third()
+    reduce_last(line, held_g, n, part_g, cot_ref)
+    reduce_sent(line, held_g, n)
+    cube.last()
+    other_ref[...] = slots[partner_ref[cube.me]]
+
+
+def exchange(part_f, part_g, partner, shards, revs):
+    slots, width = part_f.shape[0] // shards, part_f.shape[1]
+    block = (slots, width, KX)
+    vmem = pl.BlockSpec(memory_space=pltpu.VMEM)
+    shape = jax.ShapeDtypeStruct(block, BF16)
+    return pl.pallas_call(
+        functools.partial(exchange_kernel, shards, revs),
+        out_shape=(shape, shape, shape),
+        in_specs=[pl.BlockSpec(memory_space=pltpu.SMEM), vmem, vmem],
+        out_specs=(vmem, vmem, vmem),
+        scratch_shapes=[
+            pltpu.VMEM((2, shards) + block, BF16),
+            pltpu.VMEM((2, shards) + block, BF16),
+            pltpu.VMEM((revs,) + block, BF16),
+            pltpu.SemaphoreType.DMA((2, 2 * shards)),
+            pltpu.SemaphoreType.DMA((2, 2 * shards)),
+            pltpu.SemaphoreType.DMA((8,)),
+            pltpu.SemaphoreType.DMA((8,)),
+        ],
+        compiler_params=pltpu.CompilerParams(
+            collective_id=0, has_side_effects=True, vmem_limit_bytes=40 << 20
+        ),
+    )(partner, part_f.reshape((shards,) + block), part_g.reshape((shards,) + block))
+
+
+def finish_kernel(
+    n, revs, partner_ref, own_ref, other_ref, sums_ref, all_ref, total_ref, slots, gathered,
+    small, small_rows, line_send, line_recv, cube_send, cube_recv, small_send, small_recv,
+):
+    greet(n, True)
+    line = Line(n, line_send, line_recv)
+    cube = Cube(slots, cube_send, cube_recv)
+    rev, me = cube.me, line.me
+    slots[rev] = other_ref[...]
+    cube.first()
+    small[0] = sums_ref[...]
+    for i, axis in enumerate(("x", "y", "c")):
+        copy = pltpu.make_async_remote_copy(
+            src_ref=small.at[i],
+            dst_ref=small.at[4 + i],
+            send_sem=small_send.at[i],
+            recv_sem=small_recv.at[i],
+            device_id={"rev": rev + cube.step[axis]},
+            device_id_type=MESH,
+        )
+        copy.start()
+        copy.wait_recv()
+        small[i + 1] = small[i] + small[4 + i]
+        copy.wait_send()
+    small_rows[me] = small[3]
+    cube.second()
+    cube.third()
+    cube.last()
+    total = own_ref[...].astype(F32) + slots[partner_ref[rev]].astype(F32)
+    gathered[me] = total.astype(BF16)
+    for t in range(n):
+        for side in (0, 1):
+            place = me if side == 0 else n - 1 - me
+            slot = me - t if side == 0 else me + t
+            old = me - t + 1 if side == 0 else me + t - 1
+            if t > 0:
+
+                @pl.when(place >= t)
+                def _(side=side, slot=slot):
+                    line.copy(side, slot, gathered.at[slot], gathered.at[slot]).wait_recv()
+                    line.copy(
+                        side, n + slot, small_rows.at[slot], small_rows.at[slot]
+                    ).wait_recv()
+
+                @pl.when((place >= t - 1) & (place < n - 1))
+                def _(side=side, old=old):
+                    line.copy(side, old, gathered.at[old], gathered.at[old]).wait_send()
+                    line.copy(side, n + old, small_rows.at[old], small_rows.at[old]).wait_send()
+
+            if t < n - 1:
+
+                @pl.when((place >= t) & (place < n - 1))
+                def _(side=side, slot=slot):
+                    line.copy(side, n + slot, small_rows.at[slot], small_rows.at[slot]).start()
+                    line.copy(side, slot, gathered.at[slot], gathered.at[slot]).start()
+
+    all_ref[...] = gathered[...]
+    summed = small_rows[0]
+    for i in range(1, n):
+        summed = summed + small_rows[i]
+    total_ref[...] = summed
+
+
+def finish(own, other, sums, partner, shards, revs):
+    vmem = pl.BlockSpec(memory_space=pltpu.VMEM)
+    gathered, summed = pl.pallas_call(
+        functools.partial(finish_kernel, shards, revs),
+        out_shape=(
+            jax.ShapeDtypeStruct((shards,) + own.shape, BF16),
+            jax.ShapeDtypeStruct(sums.shape, F32),
+        ),
+        in_specs=[pl.BlockSpec(memory_space=pltpu.SMEM), vmem, vmem, vmem],
+        out_specs=(vmem, vmem),
+        scratch_shapes=[
+            pltpu.VMEM((revs,) + own.shape, BF16),
+            pltpu.VMEM((shards,) + own.shape, BF16),
+            pltpu.VMEM((7,) + sums.shape, F32),
+            pltpu.VMEM((shards,) + sums.shape, F32),
+            pltpu.SemaphoreType.DMA((2, 2 * shards)),
+            pltpu.SemaphoreType.DMA((2, 2 * shards)),
+            pltpu.SemaphoreType.DMA((8,)),
+            pltpu.SemaphoreType.DMA((8,)),
+            pltpu.SemaphoreType.DMA((3,)),
+            pltpu.SemaphoreType.DMA((3,)),
+        ],
+        compiler_params=pltpu.CompilerParams(
+            collective_id=1, has_side_effects=True, vmem_limit_bytes=40 << 20
+        ),
+    )(partner, own, other, sums)
+    return gathered.reshape((shards * own.shape[0],) + own.shape[1:]), summed
+
+
 def split_rows(matrix):
     high = matrix.astype(BF16)
     low = (matrix - high.astype(F32)).astype(BF16)
@@ -252,17 +572,24 @@
         jnp.asarray(np.ascontiguousarray(inv_np)), row_rank, 0, keepdims=False
     )
 
-    def spectrum(field):
-        part = forward_partial(field, col_table, row_table, scale)
-        return lax.psum_scatter(part, "row", scatter_dimension=0, tiled=True)
-
-    spectra = spectrum(fields[0])
-    grad_spec = spectrum(out_grads[0])
+    revs = lax.axis_size("rev")
+    part_f = forward_partial(fields[0], col_table, row_table, scale)
+    part_g = forward_partial(out_grads[0], col_table, row_table, scale)
     target = partner[own_rev]
 
     def route(values):
         every = lax.all_gather(values, "rev", axis=0, tiled=False)
         return lax.dynamic_index_in_dim(every, target, 0, keepdims=False)
+
+    own_kernels = revs == 8 and shards > 1
+    if own_kernels:
+        spectra, other, grad_spec = exchange(part_f, part_g, partner, shards, revs)
+    else:
+        spectra, grad_spec = (
+            lax.psum_scatter(part, "row", scatter_dimension=0, tiled=True)
+            for part in (part_f, part_g)
+        )
+        other = route(spectra)
 
     own_real = block_matrix(weight_in[:, 0, :bs])
     own_imag = block_matrix(weight_in[:, 1, :bs])
@@ -292,19 +619,22 @@
         (row_rank * slots).reshape(1).astype(jnp.int32),
         kept_blocks[own_rev].reshape(1),
         spectra,
-        route(spectra),
+        other,
         grad_spec,
         split_rows(win_t.T),
         bias,
         split_rows(wout_t),
         split_rows(win_t),
     )
-    returned = route(other_grads)
-    total = (own_grads.astype(F32) + returned.astype(F32)).astype(BF16)
-    gathered = lax.all_gather(total, "row", axis=0, tiled=True)
+    if own_kernels:
+        gathered, summed = finish(own_grads, other_grads, sums, partner, shards, revs)
+    else:
+        total = own_grads.astype(F32) + route(other_grads).astype(F32)
+        gathered = lax.all_gather(total.astype(BF16), "row", axis=0, tiled=True)
+        summed = lax.psum(sums, ("rev", "row"))
     field_grads = inverse_field(gathered, inv_table, col_table.T, scale)
 
-    summed = lax.psum(sums, ("rev", "row")) * (1.0 / math.sqrt(lax.axis_size("rev") * KX * KY))
+    summed = summed * (1.0 / math.sqrt(revs * KX * KY))
     width = 2 * channels
     pre, cot = summed[:width], summed[width:]
 

time: 271 us -> 202 us (0.75)
  waiting for transfers between devices: 146 us -> 0 us
  Pallas kernels: 45.6 us -> 190 us
  blocking collectives: 42.4 us -> 0 us
  between operations: 15.9 us -> 0.82 us
  local copies, waits for them, and re-layouts: 17.1 us -> 9.18 us
    pallas_call x0 -> x2, Pallas kernels: none -> 148 us  [the longest x1 74 us: finish(): pl.pallas_call(functools.partial(finish_kernel, shards, revs), out_shape=...]
    reduce_scatter x2 -> x0, waiting for transfers between devices: 92.5 us -> none  [spectrum(): return lax.psum_scatter(part, 'row', scatter_dimension=0, tiled=True)]
    all_gather x3 -> x0, waiting for transfers between devices: 53.8 us -> none  [the longest x2 53 us: route(): every = lax.all_gather(values, 'rev', axis=0, tiled=False)]
    psum x1 -> x0, blocking collectives: 42.4 us -> none  [local(): lax.psum(sums, ('rev', 'row'))]
    unnamed x27 -> x17, local copies, waits for them, and re-layouts: 11.1 us -> 5.13 us
  transfers between devices with their start and end apart: 5 -> 0, of which waited for: 5 -> 0; matrix products, arithmetic and copies ran while one was open for 3% -> 0% of each run, Pallas kernels for 5% -> 0%
where the time goes in v2:
time: 202 us; the launch traced here: 201 us
  Pallas kernels  190 us (94%)
  local copies, waits for them, and re-layouts  9.18 us (5%)
    pallas_call x1, Pallas kernels, finish(): pl.pallas_call(functools.partial(finish_kernel, shards, revs), out_shape=...  74 us
    pallas_call x1, Pallas kernels, exchange(): pl.pallas_call(functools.partial(exchange_kernel, shards, revs), out_shap...  74 us
    pallas_call x2, Pallas kernels, forward_partial(): pl.pallas_call(functools.partial(forward_kernel, channels, scale), grid=(...  24.9 us
    pallas_call x1, Pallas kernels, inverse_field(): pl.pallas_call(functools.partial(inverse_kernel, channels, scale), grid=(...  12.8 us
    unnamed x17, local copies, waits for them, and re-layouts  5.13 us
    pallas_call x1, Pallas kernels, mlp(): pl.pallas_call(functools.partial(mlp_kernel, slots, group, width), grid=(...  4.47 us

profile of v2, /device:TPU:0, one launch (start us, length us, event | category | flops | bytes accessed | tf_op | source)
XLA Modules:
  0.0 201.4 jit_solution(12098090773476020228)
XLA Ops:
  0.6 1.2 dynamic_slice.10.kept_ref
  1.9 1.1 dynamic-slice_bitcast_fusion
  2.9 0.0 copy-start.1
  3.0 3.4 %copy-done.1 = bf16[1,16,256,1024]{3,2,1,0:T(8,128)(2,1)S(1)} copy-done((bf16[1,16,256,1024]{3,2,1,0:T(8,128)(2,1)S(1)}, bf16[1,16,256,1024]{3,2,1,0:T(8,128)(2,1)}, u32[]{:S(2)}) %copy-start.1) | copy-done | bytes 8388632
  6.3 0.0 copy-start.4
  6.3 1.0 copy-done.4
  7.4 0.0 copy-start.2
  7.4 12.4 %shard_map.137 = bf16[256,32,128]{2,1,0:T(8,128)(2,1)S(1)} custom-call(bf16[16,256,1024]{2,1,0:T(8,128)(2,1)S(1)} %bitcast.65, bf16[1024,256]{1,0:T(8,128)(2,1)S(1)} %copy-done.4, bf16[512,256]{1,0:T(8,128)(2,1)S(1)} %get-tuple-element.60.row_ref), custom_call_target="tpu_custom_call" | custom-call | flops 3221225472 | bytes 10485760 | tf_op jit(solution)/shard_map/pallas_call | solution.py:59
  19.8 0.0 copy-start
  19.8 0.0 copy-start.5
  19.8 0.0 copy-start.7
  19.8 0.0 copy-start.6
  19.8 0.0 copy-done.2
  19.8 0.0 copy-start.3
  19.8 12.5 %shard_map.138 = bf16[256,32,128]{2,1,0:T(8,128)(2,1)S(1)} custom-call(bf16[16,256,1024]{2,1,0:T(8,128)(2,1)S(1)} %bitcast.66, bf16[1024,256]{1,0:T(8,128)(2,1)S(1)} %copy-done.4, bf16[512,256]{1,0:T(8,128)(2,1)S(1)} %get-tuple-element.60.row_ref), custom_call_target="tpu_custom_call" | custom-call | flops 3221225472 | bytes 10485760 | tf_op jit(solution)/shard_map/pallas_call | solution.py:59
  32.3 0.0 copy-done
  32.3 74.0 %shard_map.139 = (bf16[64,32,128]{2,1,0:T(8,128)(2,1)S(1)}, bf16[64,32,128]{2,1,0:T(8,128)(2,1)S(1)}, bf16[64,32,128]{2,1,0:T(8,128)(2,1)S(1)}) custom-call(s32[8]{0:T(128)S(1)} %copy-done, bf16[4,64,32,128]{3,2,1,0:T(8,128)(2,1)S(1)} %bitcast.63, bf16[4,64,32,128]{3,2,1,0:T(8,128)(2,1)S(1)} %bitcast.64), custom_call_target="tpu_custom_call" | custom-call | tf_op jit(solution)/shard_map/pallas_call | solution.py:425
  106.3 0.0 copy-done.5
  106.3 0.1 slice_bitcast_fusion.4
  106.4 0.1 fusion.8
  106.5 0.1 subtract_convert_fusion
  106.6 0.0 copy-done.7
  106.6 0.1 pad_maximum_fusion.4
  106.7 0.1 broadcast_in_dim.4.bias_ref
  106.8 0.0 copy-done.6
  106.8 0.1 subtract_convert_fusion.1
  106.9 0.1 fusion.7
  107.0 0.1 pad_maximum_fusion.3
  107.0 0.1 copy.27.win_t_ref
  107.2 4.5 %shard_map.140 = (bf16[64,32,128]{2,1,0:T(8,128)(2,1)S(1)}, bf16[64,32,128]{2,1,0:T(8,128)(2,1)S(1)}, f32[64,128]{1,0:T(8,128)S(1)}) custom-call(s32[1]{0:T(128)} %bitcast.slot0_ref, s32[1]{0:T(128)} %dynamic_slice.10.kept_ref, bf16[64,32,128]{2,1,0:T(8,128)(2,1)S(1)} %get-tuple-element.13.own_ref, bf16[64,32,128]{2,1,0:T(8,128)(2,1)S(1)} %get-tuple-element.14.other_ref, ...), custom_call_target="tpu_custom_call" | custom-call | flops 268435456 | bytes 2621440 | tf_op jit(solution)/shard_map/pallas_call | solution.py:194
  111.6 74.0 %shard_map.141 = (bf16[4,64,32,128]{3,2,1,0:T(8,128)(2,1)S(1)}, f32[64,128]{1,0:T(8,128)S(1)}) custom-call(s32[8]{0:T(128)S(1)} %copy-done, bf16[64,32,128]{2,1,0:T(8,128)(2,1)S(1)} %get-tuple-element.16.own_ref, bf16[64,32,128]{2,1,0:T(8,128)(2,1)S(1)} %get-tuple-element.17.other_ref, f32[64,128]{1,0:T(8,128)S(1)} %get-tuple-element.18.sums_ref), custom_call_target="tpu_custom_call" | custom-call | tf_op jit(solution)/shard_map/pallas_call | solution.py:510
  185.7 0.0 copy-done.3
  185.7 12.8 %shard_map.142 = bf16[16,256,1024]{2,1,0:T(8,128)(2,1)} custom-call(bf16[256,32,128]{2,1,0:T(8,128)(2,1)S(1)} %bitcast.67, bf16[512,256]{1,0:T(8,128)(2,1)S(1)} %get-tuple-element.59.row_ref, bf16[256,1024]{1,0:T(8,128)(2,1)S(1)} %copy-done.3), custom_call_target="tpu_custom_call" | custom-call | flops 3221225472 | bytes 10485760 | tf_op jit(solution)/shard_map/pallas_call | solution.py:110
  198.5 0.1 fusion.2
  198.5 0.7 maximum_maximum_fusion.2
  199.2 0.2 slice_reduce_fusion
  199.4 0.7 transpose_reshape_squeeze.6
  200.1 0.7 copy.28
  200.7 0.6 transpose_reshape_squeeze.7
  (8 shorter events, 0.0 us)
Async XLA Ops:
  2.9 3.4 %copy-start.1 = (bf16[1,16,256,1024]{3,2,1,0:T(8,128)(2,1)S(1)}, bf16[1,16,256,1024]{3,2,1,0:T(8,128)(2,1)}, u32[]{:S(2)}) copy-start(bf16[1,16,256,1024]{3,2,1,0:T(8,128)(2,1)} %param.10) | copy-start | bytes 25165828
  6.3 1.0 copy-start.4
  7.4 12.4 %copy-start.2 = (bf16[1,16,256,1024]{3,2,1,0:T(8,128)(2,1)S(1)}, bf16[1,16,256,1024]{3,2,1,0:T(8,128)(2,1)}, u32[]{:S(2)}) copy-start(bf16[1,16,256,1024]{3,2,1,0:T(8,128)(2,1)} %param.11) | copy-start | bytes 25165828
  19.8 12.6 %copy-start = (s32[8]{0:T(128)S(1)}, s32[8]{0:T(128)}, u32[]{:S(2)}) copy-start(s32[8]{0:T(128)} %partner_ref.3) | copy-start | bytes 100
  19.8 86.6 %copy-start.5 = (f32[1,2,32,16]{2,3,1,0:T(8,128)S(1)}, f32[1,2,32,16]{2,3,1,0:T(8,128)}, u32[]{:S(2)}) copy-start(f32[1,2,32,16]{2,3,1,0:T(8,128)} %param.14) | copy-start | bytes 12292
  19.8 86.8 %copy-start.7 = (f32[1,2,16]{2,1,0:T(2,128)S(1)}, f32[1,2,16]{2,1,0:T(2,128)}, u32[]{:S(2)}) copy-start(f32[1,2,16]{2,1,0:T(2,128)} %param.15) | copy-start | bytes 388
  19.8 87.0 %copy-start.6 = (f32[1,2,16,16]{3,2,1,0:T(8,128)S(1)}, f32[1,2,16,16]{3,2,1,0:T(8,128)}, u32[]{:S(2)}) copy-start(f32[1,2,16,16]{3,2,1,0:T(8,128)} %param.16) | copy-start | bytes 6148
  19.8 165.8 %copy-start.3 = (bf16[256,1024]{1,0:T(8,128)(2,1)S(1)}, bf16[256,1024]{1,0:T(8,128)(2,1)}, u32[]{:S(2)}) copy-start(bf16[256,1024]{1,0:T(8,128)(2,1)} %constant.35.col_ref) | copy-start | bytes 1572868

commit v3 on v2

--- a/solution.py
+++ b/solution.py
@@ -36,16 +36,21 @@
     return np.ascontiguousarray(split).astype(ml_dtypes.bfloat16)
 
 
-def forward_kernel(channels, scale, x_ref, col_ref, row_ref, out_ref, held):
-    step = pl.program_id(0)
-    cols = jnp.dot(x_ref[0], col_ref[...], preferred_element_type=F32).astype(BF16)
+def forward_channel(channels, scale, values, col_ref, row_ref, held, channel):
+    cols = jnp.dot(values, col_ref[...], preferred_element_type=F32).astype(BF16)
     quads = jnp.dot(row_ref[...], cols, preferred_element_type=F32)
     real = (quads[:KY, :KX] + quads[KY:, KX:]) * scale
     imag = (quads[:KY, KX:] - quads[KY:, :KX]) * scale
-    held[pl.ds(pl.multiple_of(step * KY, KY), KY), :] = real
-    held[pl.ds(pl.multiple_of((channels + step) * KY, KY), KY), :] = imag
-
-    @pl.when(step == channels - 1)
+    held[pl.ds(pl.multiple_of(channel * KY, KY), KY), :] = real
+    held[pl.ds(pl.multiple_of((channels + channel) * KY, KY), KY), :] = imag
+
+
+def forward_kernel(channels, group, scale, x_ref, col_ref, row_ref, out_ref, held):
+    step = pl.program_id(0)
+    for i in range(group):
+        forward_channel(channels, scale, x_ref[i], col_ref, row_ref, held, step * group + i)
+
+    @pl.when(step == channels // group - 1)
     def _():
         def turn(j, carry):
             out_ref[j] = held[pl.ds(j, 2 * channels, stride=KY), :].astype(BF16)
@@ -56,19 +61,20 @@
 
 def forward_partial(field, col_table, row_table, scale):
     channels, n_rows, n_cols = field.shape
+    group = 2 if channels % 2 == 0 else 1
     return pl.pallas_call(
-        functools.partial(forward_kernel, channels, scale),
-        grid=(channels,),
+        functools.partial(forward_kernel, channels, group, scale),
+        grid=(channels // group,),
         out_shape=jax.ShapeDtypeStruct((KY, 2 * channels, KX), BF16),
         in_specs=[
-            pl.BlockSpec((1, n_rows, n_cols), lambda c: (c, 0, 0)),
+            pl.BlockSpec((group, n_rows, n_cols), lambda c: (c, 0, 0)),
             pl.BlockSpec((n_cols, 2 * KX), lambda c: (0, 0)),
             pl.BlockSpec((2 * KY, n_rows), lambda c: (0, 0)),
         ],
         out_specs=pl.BlockSpec((KY, 2 * channels, KX), lambda c: (0, 0, 0)),
         scratch_shapes=[pltpu.VMEM((2 * channels * KY, KX), F32)],
         compiler_params=pltpu.CompilerParams(
-            dimension_semantics=("arbitrary",), vmem_limit_bytes=32 << 20
+            dimension_semantics=("arbitrary",), vmem_limit_bytes=57 << 20
         ),
         cost_estimate=pl.CostEstimate(
             flops=channels * n_rows * 2 * KX * (2 * n_cols + 4 * KY),
@@ -90,33 +96,36 @@
 
         lax.fori_loop(0, KY, turn, 0, unroll=8)
 
-    real = held[pl.ds(step, KY, stride=2 * channels), :].astype(BF16)
-    imag = held[pl.ds(channels + step, KY, stride=2 * channels), :].astype(BF16)
-    pair = jnp.concatenate([real, imag], axis=1)
-    n_rows = out_ref.shape[1]
-    quads = lax.dot_general(
-        row_ref[...], pair, (((1,), (0,)), ((), ())), preferred_element_type=F32
-    )
-    rows_re = quads[:n_rows, :KX] - quads[n_rows:, KX:]
-    rows_im = quads[n_rows:, :KX] + quads[:n_rows, KX:]
-    rows = jnp.concatenate([rows_re, rows_im], axis=1).astype(BF16)
-    field = jnp.dot(rows, col_ref[...], preferred_element_type=F32) * scale
-    out_ref[0] = field.astype(BF16)
+    for i in range(out_ref.shape[0]):
+        channel = step * out_ref.shape[0] + i
+        real = held[pl.ds(channel, KY, stride=2 * channels), :].astype(BF16)
+        imag = held[pl.ds(channels + channel, KY, stride=2 * channels), :].astype(BF16)
+        pair = jnp.concatenate([real, imag], axis=1)
+        n_rows = out_ref.shape[1]
+        quads = lax.dot_general(
+            row_ref[...], pair, (((1,), (0,)), ((), ())), preferred_element_type=F32
+        )
+        rows_re = quads[:n_rows, :KX] - quads[n_rows:, KX:]
+        rows_im = quads[n_rows:, :KX] + quads[:n_rows, KX:]
+        rows = jnp.concatenate([rows_re, rows_im], axis=1).astype(BF16)
+        field = jnp.dot(rows, col_ref[...], preferred_element_type=F32) * scale
+        out_ref[i] = field.astype(BF16)
 
 
 def inverse_field(total, row_table_t, col_table_t, scale):
     channels = total.shape[1] // 2
     n_rows, n_cols = row_table_t.shape[0] // 2, col_table_t.shape[1]
+    group = 2 if channels % 2 == 0 else 1
     return pl.pallas_call(
         functools.partial(inverse_kernel, channels, scale),
-        grid=(channels,),
+        grid=(channels // group,),
         out_shape=jax.ShapeDtypeStruct((channels, n_rows, n_cols), BF16),
         in_specs=[
             pl.BlockSpec((KY, 2 * channels, KX), lambda c: (0, 0, 0)),
             pl.BlockSpec((2 * n_rows, KY), lambda c: (0, 0)),
             pl.BlockSpec((2 * KX, n_cols), lambda c: (0, 0)),
         ],
-        out_specs=pl.BlockSpec((1, n_rows, n_cols), lambda c: (c, 0, 0)),
+        out_specs=pl.BlockSpec((group, n_rows, n_cols), lambda c: (c, 0, 0)),
         scratch_shapes=[pltpu.VMEM((2 * channels * KY, KX), F32)],
         compiler_params=pltpu.CompilerParams(
             dimension_semantics=("arbitrary",), vmem_limit_bytes=32 << 20
@@ -234,8 +243,9 @@
 
 
 class Cube:
-    def __init__(self, slots, send_sems, recv_sems):
+    def __init__(self, slots, send_sems, recv_sems, base=0):
         self.slots, self.send_sems, self.recv_sems = slots, send_sems, recv_sems
+        self.base = base
         self.me = lax.axis_index("rev")
         core, x, y = self.me % 2, (self.me // 2) % 2, self.me // 4
         self.step = {"c": 1 - 2 * core, "x": 2 - 4 * x, "y": 4 - 8 * y}
@@ -248,8 +258,8 @@
         return pltpu.make_async_remote_copy(
             src_ref=block,
             dst_ref=block,
-            send_sem=self.send_sems.at[tag],
-            recv_sem=self.recv_sems.at[tag],
+            send_sem=self.send_sems.at[self.base + tag],
+            recv_sem=self.recv_sems.at[self.base + tag],
             device_id={"rev": self.me + self.step[axis]},
             device_id_type=MESH,
         )
@@ -391,18 +401,38 @@
 
 
 def exchange_kernel(
-    n, revs, partner_ref, part_f, part_g, own_ref, other_ref, cot_ref, held_f, held_g, slots,
-    line_send, line_recv, cube_send, cube_recv,
+    n, channels, scale, partner_ref, part_f, field_ref, col_ref, row_ref, own_ref, other_ref,
+    cot_ref, held_f, held_g, slots, field, spread, part_g, line_send, line_recv, cube_send,
+    cube_recv, field_sem,
 ):
+    fetch = pltpu.make_async_copy(field_ref, field, field_sem)
+    fetch.start()
     greet(n, True)
     line = Line(n, line_send, line_recv)
     cube = Cube(slots, cube_send, cube_recv)
+
+    def transform(channel, carry):
+        forward_channel(channels, scale, field[channel], col_ref, row_ref, spread, channel)
+        return carry
+
     for t in range(n - 1):
         reduce_step(line, held_f, 0, part_f, t)
+        if t == 0:
+            fetch.wait()
+        lax.fori_loop(channels * t // (n - 1), channels * (t + 1) // (n - 1), transform, 0)
+    rows = KY // n
+    for shard in range(n):
+
+        def turn(j, carry, shard=shard):
+            values = spread[pl.ds(shard * rows + j, 2 * channels, stride=KY), :]
+            part_g[shard, j] = values.astype(BF16)
+            return carry
+
+        lax.fori_loop(0, rows, turn, 0, unroll=8)
     reduce_last(line, held_f, 0, part_f, own_ref)
     slots[cube.me] = own_ref[...]
+    reduce_sent(line, held_f, 0)
     cube.first()
-    reduce_sent(line, held_f, 0)
     for t in range(n - 1):
         reduce_step(line, held_g, n, part_g, t)
         if t == 0:
@@ -417,62 +447,79 @@
     other_ref[...] = slots[partner_ref[cube.me]]
 
 
-def exchange(part_f, part_g, partner, shards, revs):
+def exchange(part_f, field_g, col_table, row_table, partner, shards, revs, scale):
     slots, width = part_f.shape[0] // shards, part_f.shape[1]
     block = (slots, width, KX)
     vmem = pl.BlockSpec(memory_space=pltpu.VMEM)
     shape = jax.ShapeDtypeStruct(block, BF16)
     return pl.pallas_call(
-        functools.partial(exchange_kernel, shards, revs),
+        functools.partial(exchange_kernel, shards, width // 2, scale),
         out_shape=(shape, shape, shape),
-        in_specs=[pl.BlockSpec(memory_space=pltpu.SMEM), vmem, vmem],
+        in_specs=[
+            pl.BlockSpec(memory_space=pltpu.SMEM), vmem, pl.BlockSpec(memory_space=pl.ANY), vmem, vmem,
+        ],
         out_specs=(vmem, vmem, vmem),
         scratch_shapes=[
             pltpu.VMEM((2, shards) + block, BF16),
             pltpu.VMEM((2, shards) + block, BF16),
             pltpu.VMEM((revs,) + block, BF16),
+            pltpu.VMEM(field_g.shape, BF16),
+            pltpu.VMEM((width * KY, KX), F32),
+            pltpu.VMEM((shards,) + block, BF16),
             pltpu.SemaphoreType.DMA((2, 2 * shards)),
             pltpu.SemaphoreType.DMA((2, 2 * shards)),
             pltpu.SemaphoreType.DMA((8,)),
             pltpu.SemaphoreType.DMA((8,)),
+            pltpu.SemaphoreType.DMA,
         ],
         compiler_params=pltpu.CompilerParams(
-            collective_id=0, has_side_effects=True, vmem_limit_bytes=40 << 20
-        ),
-    )(partner, part_f.reshape((shards,) + block), part_g.reshape((shards,) + block))
+            collective_id=0, has_side_effects=True, vmem_limit_bytes=57 << 20
+        ),
+    )(partner, part_f.reshape((shards,) + block), field_g, col_table, row_table)
 
 
 def finish_kernel(
-    n, revs, partner_ref, own_ref, other_ref, sums_ref, all_ref, total_ref, slots, gathered,
-    small, small_rows, line_send, line_recv, cube_send, cube_recv, small_send, small_recv,
+    n, revs, partner_ref, own_ref, other_ref, sums_ref, all_ref, total_ref, slots_a,
+    slots_b, gathered, small, small_rows, line_send, line_recv, cube_send, cube_recv, small_send, small_recv,
 ):
     greet(n, True)
     line = Line(n, line_send, line_recv)
-    cube = Cube(slots, cube_send, cube_recv)
-    rev, me = cube.me, line.me
-    slots[rev] = other_ref[...]
-    cube.first()
+    half = own_ref.shape[0] // 2
+    buffers = (slots_a, slots_b)
+    cubes = [Cube(buffers[h], cube_send, cube_recv, 8 * h) for h in (0, 1)]
+    rev, me = cubes[0].me, line.me
+    for h in (0, 1):
+        buffers[h][rev] = other_ref[h * half : (h + 1) * half]
     small[0] = sums_ref[...]
-    for i, axis in enumerate(("x", "y", "c")):
-        copy = pltpu.make_async_remote_copy(
+
+    def small_copy(i):
+        return pltpu.make_async_remote_copy(
             src_ref=small.at[i],
             dst_ref=small.at[4 + i],
             send_sem=small_send.at[i],
             recv_sem=small_recv.at[i],
-            device_id={"rev": rev + cube.step[axis]},
+            device_id={"rev": rev + cubes[0].step["xyc"[i]]},
             device_id_type=MESH,
         )
-        copy.start()
-        copy.wait_recv()
+
+    def small_add(i):
+        small_copy(i).wait_recv()
         small[i + 1] = small[i] + small[4 + i]
-        copy.wait_send()
-    small_rows[me] = small[3]
-    cube.second()
-    cube.third()
-    cube.last()
-    total = own_ref[...].astype(F32) + slots[partner_ref[rev]].astype(F32)
-    gathered[me] = total.astype(BF16)
-    for t in range(n):
+
+    def add_half(h):
+        part = pl.ds(h * half, half)
+        other = buffers[h][partner_ref[rev]]
+        gathered[me, part] = (own_ref[part].astype(F32) + other.astype(F32)).astype(BF16)
+
+    def row_copies(side, slot, h):
+        block = gathered.at[slot, pl.ds(h * half, half)]
+        copies = [line.copy(side, h * n + slot, block, block)]
+        if h == 0:
+            few = small_rows.at[slot]
+            copies.insert(0, line.copy(side, 2 * n + slot, few, few))
+        return copies
+
+    def row_step(t, h):
         for side in (0, 1):
             place = me if side == 0 else n - 1 - me
             slot = me - t if side == 0 else me + t
@@ -481,22 +528,45 @@
 
                 @pl.when(place >= t)
                 def _(side=side, slot=slot):
-                    line.copy(side, slot, gathered.at[slot], gathered.at[slot]).wait_recv()
-                    line.copy(
-                        side, n + slot, small_rows.at[slot], small_rows.at[slot]
-                    ).wait_recv()
+                    for copy in row_copies(side, slot, h):
+                        copy.wait_recv()
 
                 @pl.when((place >= t - 1) & (place < n - 1))
                 def _(side=side, old=old):
-                    line.copy(side, old, gathered.at[old], gathered.at[old]).wait_send()
-                    line.copy(side, n + old, small_rows.at[old], small_rows.at[old]).wait_send()
+                    for copy in row_copies(side, old, h):
+                        copy.wait_send()
 
             if t < n - 1:
 
                 @pl.when((place >= t) & (place < n - 1))
                 def _(side=side, slot=slot):
-                    line.copy(side, n + slot, small_rows.at[slot], small_rows.at[slot]).start()
-                    line.copy(side, slot, gathered.at[slot], gathered.at[slot]).start()
+                    for copy in row_copies(side, slot, h):
+                        copy.start()
+
+    small_copy(0).start()
+    cubes[0].first()
+    small_add(0)
+    small_copy(1).start()
+    cubes[0].second()
+    cubes[1].first()
+    small_add(1)
+    small_copy(2).start()
+    cubes[0].third()
+    small_add(2)
+    small_rows[me] = small[3]
+    cubes[0].last()
+    for i in range(3):
+        small_copy(i).wait_send()
+    add_half(0)
+    row_step(0, 0)
+    cubes[1].second()
+    cubes[1].third()
+    cubes[1].last()
+    add_half(1)
+    row_step(0, 1)
+    for t in range(1, n):
+        row_step(t, 0)
+        row_step(t, 1)
 
     all_ref[...] = gathered[...]
     summed = small_rows[0]
@@ -516,14 +586,15 @@
         in_specs=[pl.BlockSpec(memory_space=pltpu.SMEM), vmem, vmem, vmem],
         out_specs=(vmem, vmem),
         scratch_shapes=[
-            pltpu.VMEM((revs,) + own.shape, BF16),
+            pltpu.VMEM((revs, own.shape[0] // 2) + own.shape[1:], BF16),
+            pltpu.VMEM((revs, own.shape[0] // 2) + own.shape[1:], BF16),
             pltpu.VMEM((shards,) + own.shape, BF16),
             pltpu.VMEM((7,) + sums.shape, F32),
             pltpu.VMEM((shards,) + sums.shape, F32),
-            pltpu.SemaphoreType.DMA((2, 2 * shards)),
-            pltpu.SemaphoreType.DMA((2, 2 * shards)),
-            pltpu.SemaphoreType.DMA((8,)),
-            pltpu.SemaphoreType.DMA((8,)),
+            pltpu.SemaphoreType.DMA((2, 3 * shards)),
+            pltpu.SemaphoreType.DMA((2, 3 * shards)),
+            pltpu.SemaphoreType.DMA((16,)),
+            pltpu.SemaphoreType.DMA((16,)),
             pltpu.SemaphoreType.DMA((3,)),
             pltpu.SemaphoreType.DMA((3,)),
         ],
@@ -567,14 +638,10 @@
     row_np = row_tables(n_rows, shards)
     col_table = jnp.asarray(col_np)
     row_table = lax.dynamic_index_in_dim(jnp.asarray(row_np), row_rank, 0, keepdims=False)
-    inv_np = row_np.reshape(shards, 2, KY, rows).transpose(0, 1, 3, 2).reshape(shards, 2 * rows, KY)
-    inv_table = lax.dynamic_index_in_dim(
-        jnp.asarray(np.ascontiguousarray(inv_np)), row_rank, 0, keepdims=False
-    )
+    inv_table = row_table.reshape(2, KY, rows).transpose(0, 2, 1).reshape(2 * rows, KY)
 
     revs = lax.axis_size("rev")
     part_f = forward_partial(fields[0], col_table, row_table, scale)
-    part_g = forward_partial(out_grads[0], col_table, row_table, scale)
     target = partner[own_rev]
 
     def route(values):
@@ -583,8 +650,11 @@
 
     own_kernels = revs == 8 and shards > 1
     if own_kernels:
-        spectra, other, grad_spec = exchange(part_f, part_g, partner, shards, revs)
+        spectra, other, grad_spec = exchange(
+            part_f, out_grads[0], col_table, row_table, partner, shards, revs, scale
+        )
     else:
+        part_g = forward_partial(out_grads[0], col_table, row_table, scale)
         spectra, grad_spec = (
             lax.psum_scatter(part, "row", scatter_dimension=0, tiled=True)
             for part in (part_f, part_g)

time: 202 us -> 177 us (0.88)
  Pallas kernels: 190 us -> 166 us
    pallas_call x1, Pallas kernels: 74 us -> 60.4 us  [finish(): pl.pallas_call(functools.partial(finish_kernel, shards, revs), out_shape=...]
    pallas_call x3 -> x2, Pallas kernels: 98.9 us -> 91.3 us  [the longest x1 76.3 us: exchange(): pl.pallas_call(functools.partial(exchange_kernel, shards, width // 2, sca...]
    pallas_call x1, Pallas kernels: 12.8 us -> 9.58 us  [inverse_field(): pl.pallas_call(functools.partial(inverse_kernel, channels, scale), grid=(...]
where the time goes in v3:
time: 177 us; the launch traced here: 176 us
  Pallas kernels  166 us (94%)
  local copies, waits for them, and re-layouts  8.65 us (5%)
    pallas_call x1, Pallas kernels, exchange(): pl.pallas_call(functools.partial(exchange_kernel, shards, width // 2, sca...  76.3 us
    pallas_call x1, Pallas kernels, finish(): pl.pallas_call(functools.partial(finish_kernel, shards, revs), out_shape=...  60.4 us
    pallas_call x1, Pallas kernels, forward_partial(): pl.pallas_call(functools.partial(forward_kernel, channels, group, scale),...  15 us
    pallas_call x1, Pallas kernels, inverse_field(): pl.pallas_call(functools.partial(inverse_kernel, channels, scale), grid=(...  9.58 us
    pallas_call x1, Pallas kernels, mlp(): pl.pallas_call(functools.partial(mlp_kernel, slots, group, width), grid=(...  4.46 us
    unnamed x17, local copies, waits for them, and re-layouts  3.83 us

profile of v3, /device:TPU:0, one launch (start us, length us, event | category | flops | bytes accessed | tf_op | source)
XLA Modules:
  0.0 176.4 jit_solution(14114250416285049392)
XLA Ops:
  0.6 1.2 dynamic_slice.7.kept_ref
  1.9 1.7 constant_dynamic-slice_fusion
  3.6 15.0 %shard_map.128 = bf16[256,32,128]{2,1,0:T(8,128)(2,1)} custom-call(bf16[16,256,1024]{2,1,0:T(8,128)(2,1)} %bitcast.69, bf16[1024,256]{1,0:T(8,128)(2,1)} %constant.26.clone.col_ref, bf16[512,256]{1,0:T(8,128)(2,1)} %get-tuple-element.44.row_ref), custom_call_target="tpu_custom_call" | custom-call | flops 3221225472 | bytes 10485760 | tf_op jit(solution)/shard_map/pallas_call | solution.py:65
  18.5 0.0 copy-start.5
  18.5 0.0 copy-start.7
  18.5 0.0 copy-start.6
  18.5 0.0 copy-start.3
  18.6 0.0 copy-start.4
  18.6 76.3 %shard_map.129 = (bf16[64,32,128]{2,1,0:T(8,128)(2,1)}, bf16[64,32,128]{2,1,0:T(8,128)(2,1)}, bf16[64,32,128]{2,1,0:T(8,128)(2,1)}) custom-call(s32[8]{0:T(128)} %partner_ref.3, bf16[4,64,32,128]{3,2,1,0:T(8,128)(2,1)} %bitcast.67, bf16[16,256,1024]{2,1,0:T(8,128)(2,1)} %bitcast.66, bf16[1024,256]{1,0:T(8,128)(2,1)} %constant.26.clone.col_ref, ...), custom_call_target="tpu_custom_call" | custom-call | tf_op jit(solution)/shard_map/pallas_call | solution.py:455
  94.9 0.0 copy-done.5
  94.9 0.1 slice_bitcast_fusion.4
  95.0 0.1 fusion.8
  95.0 0.1 subtract_convert_fusion
  95.2 0.0 copy-done.7
  95.2 0.1 pad_maximum_fusion.4
  95.3 0.1 broadcast_in_dim.4.bias_ref
  95.3 0.0 copy-done.6
  95.3 0.1 subtract_convert_fusion.1
  95.4 0.1 fusion.7
  95.5 0.1 pad_maximum_fusion.3
  95.6 0.1 copy.27.win_t_ref
  95.7 0.0 copy-start
  95.7 1.0 copy-done
  96.8 0.0 copy-start.1
  96.8 1.0 copy-done.1
  97.8 0.0 copy-start.2
  97.8 1.0 copy-done.2
  98.9 4.5 %shard_map.130 = (bf16[64,32,128]{2,1,0:T(8,128)(2,1)S(1)}, bf16[64,32,128]{2,1,0:T(8,128)(2,1)S(1)}, f32[64,128]{1,0:T(8,128)S(1)}) custom-call(s32[1]{0:T(128)} %bitcast.slot0_ref, s32[1]{0:T(128)} %dynamic_slice.7.kept_ref, bf16[64,32,128]{2,1,0:T(8,128)(2,1)S(1)} %copy-done, bf16[64,32,128]{2,1,0:T(8,128)(2,1)S(1)} %copy-done.1, ...), custom_call_target="tpu_custom_call" | custom-call | flops 268435456 | bytes 2621440 | tf_op jit(solution)/shard_map/pallas_call | solution.py:203
  103.3 0.0 copy-done.3
  103.3 60.4 %shard_map.131 = (bf16[4,64,32,128]{3,2,1,0:T(8,128)(2,1)S(1)}, f32[64,128]{1,0:T(8,128)S(1)}) custom-call(s32[8]{0:T(128)S(1)} %copy-done.3, bf16[64,32,128]{2,1,0:T(8,128)(2,1)S(1)} %get-tuple-element.16.own_ref, bf16[64,32,128]{2,1,0:T(8,128)(2,1)S(1)} %get-tuple-element.17.other_ref, f32[64,128]{1,0:T(8,128)S(1)} %get-tuple-element.18.sums_ref), custom_call_target="tpu_custom_call" | custom-call | tf_op jit(solution)/shard_map/pallas_call | solution.py:580
  163.7 0.1 copy.28
  163.8 0.0 copy-done.4
  163.9 9.6 %shard_map.132 = bf16[16,256,1024]{2,1,0:T(8,128)(2,1)} custom-call(bf16[256,32,128]{2,1,0:T(8,128)(2,1)S(1)} %bitcast.65, bf16[512,256]{1,0:T(8,128)(2,1)S(1)} %bitcast.64, bf16[256,1024]{1,0:T(8,128)(2,1)S(1)} %copy-done.4), custom_call_target="tpu_custom_call" | custom-call | flops 3221225472 | bytes 10485760 | tf_op jit(solution)/shard_map/pallas_call | solution.py:119
  173.4 0.1 fusion.2
  173.5 0.7 maximum_maximum_fusion.2
  174.2 0.2 slice_reduce_fusion
  174.4 0.7 transpose_reshape_squeeze.6
  175.1 0.7 copy.29
  175.7 0.6 transpose_reshape_squeeze.7
  (8 shorter events, 0.0 us)
Async XLA Ops:
  18.5 76.4 %copy-start.5 = (f32[1,2,32,16]{2,3,1,0:T(8,128)S(1)}, f32[1,2,32,16]{2,3,1,0:T(8,128)}, u32[]{:S(2)}) copy-start(f32[1,2,32,16]{2,3,1,0:T(8,128)} %param.13) | copy-start | bytes 12292
  18.5 76.6 %copy-start.7 = (f32[1,2,16]{2,1,0:T(2,128)S(1)}, f32[1,2,16]{2,1,0:T(2,128)}, u32[]{:S(2)}) copy-start(f32[1,2,16]{2,1,0:T(2,128)} %param.14) | copy-start | bytes 388
  18.5 76.8 %copy-start.6 = (f32[1,2,16,16]{3,2,1,0:T(8,128)S(1)}, f32[1,2,16,16]{3,2,1,0:T(8,128)}, u32[]{:S(2)}) copy-start(f32[1,2,16,16]{3,2,1,0:T(8,128)} %param.15) | copy-start | bytes 6148
  18.5 84.8 %copy-start.3 = (s32[8]{0:T(128)S(1)}, s32[8]{0:T(128)}, u32[]{:S(2)}) copy-start(s32[8]{0:T(128)} %partner_ref.3) | copy-start | bytes 100
  18.6 145.3 %copy-start.4 = (bf16[256,1024]{1,0:T(8,128)(2,1)S(1)}, bf16[256,1024]{1,0:T(8,128)(2,1)}, u32[]{:S(2)}) copy-start(bf16[256,1024]{1,0:T(8,128)(2,1)} %constant.30.col_ref) | copy-start | bytes 1572868
  95.7 1.1 copy-start
  96.8 1.0 copy-start.1
  97.8 1.0 copy-start.2

commit v4 on v3

--- a/solution.py
+++ b/solution.py
@@ -61,7 +61,7 @@
 
 def forward_partial(field, col_table, row_table, scale):
     channels, n_rows, n_cols = field.shape
-    group = 2 if channels % 2 == 0 else 1
+    group = 4 if channels % 4 == 0 else 1
     return pl.pallas_call(
         functools.partial(forward_kernel, channels, group, scale),
         grid=(channels // group,),
@@ -115,7 +115,7 @@
 def inverse_field(total, row_table_t, col_table_t, scale):
     channels = total.shape[1] // 2
     n_rows, n_cols = row_table_t.shape[0] // 2, col_table_t.shape[1]
-    group = 2 if channels % 2 == 0 else 1
+    group = 4 if channels % 4 == 0 else 1
     return pl.pallas_call(
         functools.partial(inverse_kernel, channels, scale),
         grid=(channels // group,),
@@ -473,7 +473,7 @@
             pltpu.SemaphoreType.DMA,
         ],
         compiler_params=pltpu.CompilerParams(
-            collective_id=0, has_side_effects=True, vmem_limit_bytes=57 << 20
+            collective_id=0, has_side_effects=True, vmem_limit_bytes=44 << 20
         ),
     )(partner, part_f.reshape((shards,) + block), field_g, col_table, row_table)
 

time: 177 us -> 174 us (0.983)
  Pallas kernels: 166 us -> 162 us
    pallas_call x1, Pallas kernels: 76.3 us -> 73.9 us  [exchange(): pl.pallas_call(functools.partial(exchange_kernel, shards, width // 2, sca...]
    unnamed x17 -> x21, local copies, waits for them, and re-layouts: 3.83 us -> 5.19 us
where the time goes in v4:
time: 174 us
  Pallas kernels  162 us (93%)
  local copies, waits for them, and re-layouts  10 us (6%)
    pallas_call x1, Pallas kernels, exchange(): pl.pallas_call(functools.partial(exchange_kernel, shards, width // 2, sca...  73.9 us
    pallas_call x1, Pallas kernels, finish(): pl.pallas_call(functools.partial(finish_kernel, shards, revs), out_shape=...  59.9 us
    pallas_call x1, Pallas kernels, forward_partial(): pl.pallas_call(functools.partial(forward_kernel, channels, group, scale),...  14.7 us
    pallas_call x1, Pallas kernels, inverse_field(): pl.pallas_call(functools.partial(inverse_kernel, channels, scale), grid=(...  8.66 us
    unnamed x21, local copies, waits for them, and re-layouts  5.19 us
    pallas_call x1, Pallas kernels, mlp(): pl.pallas_call(functools.partial(mlp_kernel, slots, group, width), grid=(...  4.47 us

profile of v4, /device:TPU:0, one launch (start us, length us, event | category | flops | bytes accessed | tf_op | source)
XLA Modules:
  0.0 173.7 jit_solution(10360123709745033024)
XLA Ops:
  0.6 0.0 copy-start.2
  0.6 0.0 copy-start.3
  0.7 1.3 dynamic_slice.7.kept_ref
  2.0 1.7 constant_dynamic-slice_fusion
  3.6 0.0 copy-start.1
  3.6 0.0 copy-start.7
  3.6 0.0 copy-start.8
  3.6 0.0 copy-start.6
  3.6 14.7 %shard_map.128 = bf16[256,32,128]{2,1,0:T(8,128)(2,1)} custom-call(bf16[16,256,1024]{2,1,0:T(8,128)(2,1)} %bitcast.69, bf16[1024,256]{1,0:T(8,128)(2,1)} %constant.26.clone.col_ref, bf16[512,256]{1,0:T(8,128)(2,1)} %get-tuple-element.44.row_ref), custom_call_target="tpu_custom_call" | custom-call | flops 3221225472 | bytes 10485760 | tf_op jit(solution)/shard_map/pallas_call | solution.py:65
  18.3 0.0 copy-start.9
  18.3 0.0 copy-done.2
  18.3 0.0 copy-done.3
  18.3 0.0 copy-done.1
  18.3 0.0 copy-start
  18.3 1.6 copy-done
  19.9 73.9 %shard_map.129 = (bf16[64,32,128]{2,1,0:T(8,128)(2,1)S(1)}, bf16[64,32,128]{2,1,0:T(8,128)(2,1)S(1)}, bf16[64,32,128]{2,1,0:T(8,128)(2,1)S(1)}) custom-call(s32[8]{0:T(128)S(1)} %copy-done.3, bf16[4,64,32,128]{3,2,1,0:T(8,128)(2,1)S(1)} %bitcast.64, bf16[16,256,1024]{2,1,0:T(8,128)(2,1)} %bitcast.67, bf16[1024,256]{1,0:T(8,128)(2,1)S(1)} %copy-done.2, ...), custom_call_target="tpu_custom_call" | custom-call | tf_op jit(solution)/shard_map/pallas_call | solution.py:455
  93.8 0.0 copy-done.7
  93.8 0.1 slice_bitcast_fusion.4
  93.9 0.1 fusion.8
  94.0 0.1 subtract_convert_fusion
  94.1 0.0 copy-done.9
  94.1 0.1 pad_maximum_fusion.4
  94.2 0.1 broadcast_in_dim.4.bias_ref
  94.2 0.0 copy-done.8
  94.3 0.1 subtract_convert_fusion.1
  94.3 0.1 fusion.7
  94.4 0.1 pad_maximum_fusion.3
  94.5 0.1 copy.27.win_t_ref
  94.6 4.5 %shard_map.130 = (bf16[64,32,128]{2,1,0:T(8,128)(2,1)S(1)}, bf16[64,32,128]{2,1,0:T(8,128)(2,1)S(1)}, f32[64,128]{1,0:T(8,128)S(1)}) custom-call(s32[1]{0:T(128)} %bitcast.slot0_ref, s32[1]{0:T(128)} %dynamic_slice.7.kept_ref, bf16[64,32,128]{2,1,0:T(8,128)(2,1)S(1)} %get-tuple-element.13.own_ref, bf16[64,32,128]{2,1,0:T(8,128)(2,1)S(1)} %get-tuple-element.14.other_ref, ...), custom_call_target="tpu_custom_call" | custom-call | flops 268435456 | bytes 2621440 | tf_op jit(solution)/shard_map/pallas_call | solution.py:203
  99.1 59.9 %shard_map.131 = (bf16[4,64,32,128]{3,2,1,0:T(8,128)(2,1)S(1)}, f32[64,128]{1,0:T(8,128)S(1)}) custom-call(s32[8]{0:T(128)S(1)} %copy-done.3, bf16[64,32,128]{2,1,0:T(8,128)(2,1)S(1)} %get-tuple-element.16.own_ref, bf16[64,32,128]{2,1,0:T(8,128)(2,1)S(1)} %get-tuple-element.17.other_ref, f32[64,128]{1,0:T(8,128)S(1)} %get-tuple-element.18.sums_ref), custom_call_target="tpu_custom_call" | custom-call | tf_op jit(solution)/shard_map/pallas_call | solution.py:580
  159.1 0.0 copy-start.4
  159.1 1.3 copy-done.4
  160.4 0.1 copy.28
  160.5 0.0 copy-done.6
  160.5 0.0 copy-start.5
  160.5 1.6 copy-done.5
  162.1 8.7 %shard_map.132 = bf16[16,256,1024]{2,1,0:T(8,128)(2,1)} custom-call(bf16[256,32,128]{2,1,0:T(8,128)(2,1)S(1)} %bitcast.66, bf16[512,256]{1,0:T(8,128)(2,1)S(1)} %bitcast.65, bf16[256,1024]{1,0:T(8,128)(2,1)S(1)} %copy-done.6), custom_call_target="tpu_custom_call" | custom-call | flops 3221225472 | bytes 10485760 | tf_op jit(solution)/shard_map/pallas_call | solution.py:119
  170.8 0.1 fusion.2
  170.9 0.7 maximum_maximum_fusion.2
  171.6 0.2 slice_reduce_fusion
  171.7 0.7 transpose_reshape_squeeze.6
  172.4 0.7 copy.29
  173.1 0.6 transpose_reshape_squeeze.7
  (8 shorter events, 0.0 us)
Async XLA Ops:
  0.6 17.7 %copy-start.2 = (bf16[1024,256]{1,0:T(8,128)(2,1)S(1)}, bf16[1024,256]{1,0:T(8,128)(2,1)}, u32[]{:S(2)}) copy-start(bf16[1024,256]{1,0:T(8,128)(2,1)} %constant.26.clone.col_ref) | copy-start | bytes 1572868
  0.6 17.7 %copy-start.3 = (s32[8]{0:T(128)S(1)}, s32[8]{0:T(128)}, u32[]{:S(2)}) copy-start(s32[8]{0:T(128)} %partner_ref.3) | copy-start | bytes 100
  3.6 14.7 %copy-start.1 = (bf16[512,256]{1,0:T(8,128)(2,1)S(1)}, bf16[512,256]{1,0:T(8,128)(2,1)}, u32[]{:S(2)}) copy-start(bf16[512,256]{1,0:T(8,128)(2,1)} %get-tuple-element.44.row_ref) | copy-start | bytes 786436
  3.6 90.2 %copy-start.7 = (f32[1,2,32,16]{2,3,1,0:T(8,128)S(1)}, f32[1,2,32,16]{2,3,1,0:T(8,128)}, u32[]{:S(2)}) copy-start(f32[1,2,32,16]{2,3,1,0:T(8,128)} %param.13) | copy-start | bytes 12292
  3.6 90.6 %copy-start.8 = (f32[1,2,16,16]{3,2,1,0:T(8,128)S(1)}, f32[1,2,16,16]{3,2,1,0:T(8,128)}, u32[]{:S(2)}) copy-start(f32[1,2,16,16]{3,2,1,0:T(8,128)} %param.15) | copy-start | bytes 6148
  3.6 156.9 %copy-start.6 = (bf16[256,1024]{1,0:T(8,128)(2,1)S(1)}, bf16[256,1024]{1,0:T(8,128)(2,1)}, u32[]{:S(2)}) copy-start(bf16[256,1024]{1,0:T(8,128)(2,1)} %constant.30.col_ref) | copy-start | bytes 1572868
  18.3 75.8 %copy-start.9 = (f32[1,2,16]{2,1,0:T(2,128)S(1)}, f32[1,2,16]{2,1,0:T(2,128)}, u32[]{:S(2)}) copy-start(f32[1,2,16]{2,1,0:T(2,128)} %param.14) | copy-start | bytes 388
  18.3 1.6 copy-start
  159.1 1.3 copy-start.4
  160.5 1.6 copy-start.5
